TPU v7x, 128 devices: a whole 4x4x4 slice. The times are simulated.
128 devices in a mesh: dp: 4 (over x), gz: 32 (over y, z, core).
Axes of the slice: x: 4, y: 4, z: 4, core: 2. Of those that a mesh axis runs over, the one named last changes fastest.
Arguments:
- fields: bfloat16 [4, 256, 16, 128, 128], P('dp', 'gz'), may hold values from -6 to 6
- cotangent: bfloat16 [4, 256, 16, 128, 128], P('dp', 'gz'), may hold values from -6 to 6
- spectral_weight: bfloat16 [2, 16, 16, 32768], P(None, None, None, 'gz'), may hold values from -1.5 to 1.5
- pointwise_weight: bfloat16 [16, 16], replicated, may hold values from -1.5 to 1.5
Outputs:
- layer_output: bfloat16 [4, 256, 16, 128, 128], P('dp', 'gz')
- input_grad: bfloat16 [4, 256, 16, 128, 128], P('dp', 'gz')
- pointwise_grad: float32 [16, 16], replicated
- spectral_grad: float32 [2, 16, 16, 32768], P(None, None, None, 'gz')
All inputs are finite; a program needn't handle non-finite values.
Results may differ from a plain program's by a relative error of at most 0.001.
Values sent between devices are 32-bit elements; how exact they have to be, the bound alone decides.
A program may use at most 128 MiB of HBM per device.

v0:
```python
import math

import jax
import jax.numpy as jnp
from jax import lax
from jax.sharding import PartitionSpec as P

M = 32


HIGHEST = lax.Precision.HIGHEST


def angle_table(length, modes, first, count):
    positions = first + jnp.arange(count, dtype=jnp.int32)
    frequency = jnp.arange(modes, dtype=jnp.int32)
    phase = positions[:, None] * frequency[None, :] % length
    angles = phase.astype(jnp.float32) * (2.0 * math.pi / length)
    return (jnp.cos(angles), jnp.sin(angles))


def plane_forward(field, cos_x, sin_x, cos_y, sin_y):
    modes = cos_x.shape[1]
    section = jnp.einsum(
        "szcxy,yb->szcxb", field, jnp.concatenate([cos_y, -sin_y], axis=1), precision=HIGHEST
    )
    block = jnp.einsum(
        "szcxb,xa->szcab", section, jnp.concatenate([cos_x, -sin_x], axis=1), precision=HIGHEST
    )
    real_part = block[..., :modes, :modes] - block[..., modes:, modes:]
    imag_part = block[..., :modes, modes:] + block[..., modes:, :modes]
    shape = real_part.shape[:3] + (modes * modes,)
    return jnp.stack([real_part.reshape(shape), imag_part.reshape(shape)])


def depth_forward(planes, cos_z, sin_z):

    def contract(values, table):
        return jnp.einsum("szcp,zk->scpk", values, table, precision=HIGHEST)

    real_out = contract(planes[0], cos_z) + contract(planes[1], sin_z)
    imag_out = contract(planes[1], cos_z) - contract(planes[0], sin_z)
    shape = real_out.shape[:2] + (real_out.shape[2] * real_out.shape[3],)
    return jnp.stack([real_out.reshape(shape), imag_out.reshape(shape)])


def depth_inverse(spectrum, cos_z, sin_z):
    modes = cos_z.shape[1]
    shape = spectrum.shape[1:3] + (spectrum.shape[3] // modes, modes)
    real_in = spectrum[0].reshape(shape)
    imag_in = spectrum[1].reshape(shape)

    def expand(values, table):
        return jnp.einsum("scpk,zk->szcp", values, table, precision=HIGHEST)

    real_out = expand(real_in, cos_z) - expand(imag_in, sin_z)
    imag_out = expand(real_in, sin_z) + expand(imag_in, cos_z)
    return jnp.stack([real_out, imag_out])


def plane_inverse(planes, cos_x, sin_x, cos_y, sin_y):
    modes = cos_x.shape[1]
    shape = planes.shape[1:4] + (modes, modes)
    real_in = planes[0].reshape(shape)
    imag_in = planes[1].reshape(shape)

    def spread(values, table):
        return jnp.einsum("szcab,xa->szcxb", values, table, precision=HIGHEST)

    real_mid = spread(real_in, cos_x) - spread(imag_in, sin_x)
    imag_mid = spread(real_in, sin_x) + spread(imag_in, cos_x)
    joined = jnp.concatenate([real_mid, imag_mid], axis=-1)
    return jnp.einsum(
        "szcxb,yb->szcxy", joined, jnp.concatenate([cos_y, -sin_y], axis=1), precision=HIGHEST
    )


def mix_modes(spectrum, weight):

    def term(values, table):
        return jnp.einsum("scm,com->som", values, table, precision=HIGHEST)

    real_out = term(spectrum[0], weight[0]) - term(spectrum[1], weight[1])
    imag_out = term(spectrum[0], weight[1]) + term(spectrum[1], weight[0])
    return jnp.stack([real_out, imag_out])


def mix_adjoint(grad_spec, weight):

    def term(values, table):
        return jnp.einsum("som,com->scm", values, table, precision=HIGHEST)

    real_out = term(grad_spec[0], weight[0]) + term(grad_spec[1], weight[1])
    imag_out = term(grad_spec[1], weight[0]) - term(grad_spec[0], weight[1])
    return jnp.stack([real_out, imag_out])


def mix_weight_grad(spectrum, grad_spec):

    def term(values, other):
        return jnp.einsum("scm,som->com", values, other, precision=HIGHEST)

    real_out = term(spectrum[0], grad_spec[0]) + term(spectrum[1], grad_spec[1])
    imag_out = term(spectrum[0], grad_spec[1]) - term(spectrum[1], grad_spec[0])
    return jnp.stack([real_out, imag_out])


def gelu_tanh(values):
    return jax.nn.gelu(values, approximate=True)


def shards(fields, cotangent, spectral_weight, pointwise_weight):
    groups = lax.axis_size("gz")
    depth_here = fields.shape[1]
    width_x = fields.shape[3]
    width_y = fields.shape[4]
    depth_all = depth_here * groups
    first = lax.axis_index("gz") * depth_here
    total_modes = M * M * M
    scale = 1.0 / math.sqrt(width_x * width_y * depth_all * total_modes)
    cells = lax.axis_size("dp") * fields.shape[0] * width_x * width_y * depth_all
    cos_x, sin_x = angle_table(width_x, M, 0, width_x)
    cos_y, sin_y = angle_table(width_y, M, 0, width_y)
    cos_near, sin_near = angle_table(depth_all, M, first, depth_here)
    weight = spectral_weight.astype(jnp.float32)
    inputs = fields.astype(jnp.float32)
    planes = plane_forward(inputs, cos_x, sin_x, cos_y, sin_y)
    partial_value = depth_forward(planes, cos_near, sin_near)
    input_spec = lax.psum_scatter(partial_value, "gz", scatter_dimension=3, tiled=True)
    mixed = mix_modes(input_spec, weight)
    whole = lax.all_gather(mixed, "gz", axis=3, tiled=True)
    back_planes = depth_inverse(whole, cos_near, sin_near)
    spectral = plane_inverse(back_planes, cos_x, sin_x, cos_y, sin_y) * scale
    pointwise = jnp.einsum(
        "szcxy,co->szoxy", fields, pointwise_weight, preferred_element_type=jnp.float32
    )
    pre = spectral + pointwise
    activation, pullback = jax.vjp(gelu_tanh, pre)
    grad_pre = pullback(cotangent.astype(jnp.float32))[0]
    grad_planes = plane_forward(grad_pre, cos_x, sin_x, cos_y, sin_y)
    grad_partial = depth_forward(grad_planes, cos_near, sin_near)
    grad_spec = lax.psum_scatter(grad_partial, "gz", scatter_dimension=3, tiled=True) * scale
    adjoint = mix_adjoint(grad_spec, weight)
    adjoint_whole = lax.all_gather(adjoint, "gz", axis=3, tiled=True)
    adjoint_planes = depth_inverse(adjoint_whole, cos_near, sin_near)
    back = plane_inverse(adjoint_planes, cos_x, sin_x, cos_y, sin_y)
    mixing = pointwise_weight.astype(jnp.float32)
    grad_input = back + jnp.einsum("szoxy,co->szcxy", grad_pre, mixing, precision=HIGHEST)
    point_term = jnp.einsum("szcxy,szoxy->co", inputs, grad_pre, precision=HIGHEST)
    spec_term = mix_weight_grad(input_spec, grad_spec)
    point_total = lax.psum(point_term, ("dp", "gz"))
    spec_total = lax.psum(spec_term, "dp")
    pointwise_grad = point_total * (1.0 / math.sqrt(cells))
    spectral_grad = spec_total * math.sqrt(total_modes / cells)
    return (
        activation.astype(jnp.bfloat16),
        grad_input.astype(jnp.bfloat16),
        pointwise_grad,
        spectral_grad,
    )


def solution(mesh):
    placed = (
        P("dp", "gz", None, None, None),
        P("dp", "gz", None, None, None),
        P(None, None, None, "gz"),
        P(),
    )
    return jax.shard_map(
        shards,
        mesh=mesh,
        in_specs=placed,
        out_specs=(
            P("dp", "gz", None, None, None),
            P("dp", "gz", None, None, None),
            P(),
            P(None, None, None, "gz"),
        ),
        check_vma=False,
    )
```

profile of v0, /device:TPU:1, one launch (start us, length us, event | category | flops | bytes accessed | tf_op | source)
XLA Modules:
  0.0 663.1 jit_solution(1952883024339252193)
XLA Ops:
  7.3 6.2 fusion.132
  13.5 12.2 %fusion.26 = f32[1,8,16,64,64]{4,3,2,1,0:T(8,128)S(1)} fusion(f32[64,8,16,128]{3,0,2,1:T(8,128)S(1)} %fusion.132, f32[128,32]{0,1:T(8,128)S(1)} %get-tuple-element.45, f32[128,32]{0,1:T(8,128)S(1)} %get-tuple-element.44), kind=kOutput, calls=%fused_computation.37 | convolution fusion | flops 805314560 | bytes 6324224 | tf_op jit(solution)/shard_map/szcxb,xa->szcab/dot_general | solution.py:27
  25.7 2.5 slice_subtract_fusion.1
  28.1 2.6 reshape.218
  30.7 1.0 reshape.219
  31.7 2.1 fusion.72
  33.8 2.1 fusion.76
  36.0 2.4 convolution_subtract_fusion.1
  38.3 3.6 convolution_add_fusion.1
  41.9 6.2 copy.34
  48.2 7.0 %stack_reshape.12 = f32[1,1,16,32768]{3,2,1,0:T(8,128)} reshape(f32[16,1024,32]{2,1,0:T(8,128)} %copy.34) | data formatting | bytes 4194304 | tf_op jit(solution)/shard_map/stack;reshape | solution.py:44
  55.1 4.6 copy.37
  59.8 7.6 %stack_reshape.13 = f32[1,1,16,32768]{3,2,1,0:T(8,128)} reshape(f32[16,1024,32]{2,1,0:T(8,128)} %copy.37) | data formatting | bytes 4194304 | tf_op jit(solution)/shard_map/stack;reshape | solution.py:44
  67.3 4.1 pad_maximum_fusion
  71.6 84.1 %reduce-scatter.3.cloned.1.call-done = f32[2,1,16,1024]{3,2,1,0:T(8,128)} async-done(((f32[2,1,16,32768]{3,2,1,0:T(8,128)}), f32[2,1,16,1024]{3,2,1,0:T(8,128)}) %reduce-scatter.3.cloned.1.call-update) | async-done | bytes 131088 | tf_op jit(solution)/shard_map/reduce_scatter | solution.py:129
  157.7 8.0 %fusion.24 = f32[16,8,128,128]{3,0,2,1:T(8,128)} fusion(bf16[8,16,128,128]{3,2,1,0:T(8,128)(2,1)} %bitcast.272, bf16[16,16]{1,0:T(8,128)(2,1)S(1)} %copy-done), kind=kOutput, calls=%fused_computation.35 | convolution fusion | flops 67108864 | bytes 12583424 | tf_op jit(solution)/shard_map/szcxy,co->szoxy/dot_general | solution.py:134
  165.7 40.5 %all-gather.3.cloned.1.call-done = f32[2,1,16,32768]{3,2,1,0:T(8,128)} async-done(((f32[2,1,16,1024]{3,2,1,0:T(8,128)}), f32[2,1,16,32768]{3,2,1,0:T(8,128)}) %all-gather.3.cloned.1.call-update) | async-done | bytes 4194320 | tf_op jit(solution)/shard_map/all_gather | solution.py:131
  206.2 3.9 fusion.255
  210.0 5.9 reshape.222
  216.0 9.6 %fusion.113 = f32[8,16,1024]{2,0,1:T(8,128)S(1)} fusion(f32[16,1024,32]{2,1,0:T(8,128)} %reshape.222, s32[8]{0:T(128)S(1)} %iota_add_fusion), kind=kOutput, calls=%fused_computation.149 | convolution fusion | flops 50335232 | bytes 2621472 | tf_op jit(solution)/shard_map/scpk,zk->szcp/dot_general | solution.py:54
  225.6 7.2 %fusion.124 = f32[8,16,1024]{2,0,1:T(8,128)S(1)} fusion(f32[16,1024,32]{2,1,0:T(8,128)S(1)} %copy-done.2, s32[8]{0:T(128)S(1)} %iota_add_fusion), kind=kOutput, calls=%fused_computation.160 | convolution fusion | flops 50335232 | bytes 2621472 | tf_op jit(solution)/shard_map/scpk,zk->szcp/dot_general | solution.py:54
  232.8 4.9 reshape.223
  237.7 11.2 %convolution_add_fusion.3 = f32[8,16,1024]{2,0,1:T(8,128)} fusion(f32[8,16,1024]{2,0,1:T(8,128)S(1)} %fusion.113, f32[16,1024,32]{2,1,0:T(8,128)} %reshape.223, s32[8]{0:T(128)S(1)} %iota_add_fusion), kind=kOutput, calls=%fused_computation.78 | convolution fusion | flops 50466304 | bytes 3145760 | tf_op jit(solution)/shard_map/scpk,zk->szcp/dot_general | solution.py:54
  248.9 1.7 reshape.225
  250.7 4.9 fusion.37
  255.6 4.9 fusion.39
  260.4 9.6 %convolution_subtract_fusion.3 = f32[8,16,1024]{2,0,1:T(8,128)S(1)} fusion(f32[8,16,1024]{2,0,1:T(8,128)S(1)} %fusion.124, f32[16,1024,32]{2,1,0:T(8,128)} %reshape.223, s32[8]{0:T(128)S(1)} %iota_add_fusion), kind=kOutput, calls=%fused_computation.79 | convolution fusion | flops 50466304 | bytes 3145760 | tf_op jit(solution)/shard_map/scpk,zk->szcp/dot_general | solution.py:54
  270.8 5.3 subtract_bitcast_fusion.1
  276.1 3.6 add_bitcast_fusion.1
  279.6 24.5 %fusion.2 = (f32[8,16,128,128]{3,2,1,0:T(8,128)S(1)}, bf16[1,8,16,128,128]{4,3,2,1,0:T(8,128)(2,1)}) fusion(bf16[1,8,16,128,128]{4,3,2,1,0:T(8,128)(2,1)S(1)} %copy-done.10, f32[16,8,128,128]{3,0,2,1:T(8,128)} %fusion.24, f32[128,32]{0,1:T(8,128)S(1)} %get-tuple-element.45, f32[128,32]{0,1:T(8,128)S(1)} %get-tuple-element.44, ...), kind=kOutput, calls=%fused_computation.6 | convolution fusion | flops 1662001152 | bytes 29392896 | tf_op jit(solution)/shard_map/szcxb,yb->szcxy/dot_general | solution.py:73
  304.1 9.5 %fusion.131 = f32[8,16,128,64]{2,3,1,0:T(8,128)S(1)} fusion(f32[8,16,128,128]{3,2,1,0:T(8,128)S(1)} %get-tuple-element.24, f32[128,32]{0,1:T(8,128)S(1)} %get-tuple-element.45, f32[128,32]{0,1:T(8,128)S(1)} %get-tuple-element.44), kind=kOutput, calls=%fused_computation.168 | convolution fusion | flops 1610620928 | bytes 12615680 | tf_op jit(solution)/shard_map/szcxy,yb->szcxb/dot_general | solution.py:24
  313.6 12.1 %convolution_bitcast_fusion = f32[1,8,16,64,64]{4,3,2,1,0:T(8,128)S(1)} fusion(f32[8,16,128,64]{2,3,1,0:T(8,128)S(1)} %fusion.131, f32[128,32]{0,1:T(8,128)S(1)} %get-tuple-element.45, f32[128,32]{0,1:T(8,128)S(1)} %get-tuple-element.44), kind=kOutput, calls=%fused_computation.38 | convolution fusion | flops 805314560 | bytes 6324224 | tf_op jit(solution)/shard_map/szcxb,xa->szcab/dot_general | solution.py:27
  325.7 2.5 slice_subtract_fusion
  328.2 2.8 reshape.228
  331.0 1.0 reshape.229
  332.0 2.1 fusion.66
  334.1 2.1 fusion.70
  336.3 2.4 convolution_subtract_fusion
  338.7 3.6 convolution_add_fusion
  342.2 6.2 copy.51
  348.4 7.0 %stack_reshape.14 = f32[1,1,16,32768]{3,2,1,0:T(8,128)} reshape(f32[16,1024,32]{2,1,0:T(8,128)} %copy.51) | data formatting | bytes 4194304 | tf_op jit(solution)/shard_map/stack;reshape | solution.py:44
  355.4 4.7 copy.54
  360.1 7.1 %stack_reshape.15 = f32[1,1,16,32768]{3,2,1,0:T(8,128)} reshape(f32[16,1024,32]{2,1,0:T(8,128)} %copy.54) | data formatting | bytes 4194304 | tf_op jit(solution)/shard_map/stack;reshape | solution.py:44
  367.2 4.1 pad_maximum_fusion.1
  371.4 79.7 %reduce-scatter.5.cloned.1.call-done = f32[2,1,16,1024]{3,2,1,0:T(8,128)} async-done(((f32[2,1,16,32768]{3,2,1,0:T(8,128)}), f32[2,1,16,1024]{3,2,1,0:T(8,128)}) %reduce-scatter.5.cloned.1.call-update) | async-done | bytes 131088 | tf_op jit(solution)/shard_map/reduce_scatter | solution.py:142
  452.1 1.1 add_bitcast_fusion.2
  453.3 1.5 pad_maximum_fusion.2
  455.7 22.2 %fusion.53 = f32[16,16]{0,1:T(8,128)S(1)} fusion(bf16[8,16,128,128]{3,2,1,0:T(8,128)(2,1)} %bitcast.273, f32[8,16,128,128]{3,2,1,0:T(8,128)} %copy-done.1), kind=kOutput, calls=%fused_computation.80 | convolution fusion | flops 402653184 | bytes 12583936 | tf_op jit(solution)/shard_map/szcxy,szoxy->co/dot_general | solution.py:149
  477.9 66.8 %psum.14 = f32[16,16]{0,1:T(8,128)S(1)} all-reduce(f32[16,16]{0,1:T(8,128)S(1)} %fusion.53), channel_id=1, replica_groups=mesh['dp'=4,'gz'=32] {'dp','gz'}, use_global_device_ids=true, to_apply=%region_2.3 | all-reduce | flops 256 | bytes 2048 | tf_op jit(solution)/shard_map/psum | solution.py:151
  545.4 15.3 %fusion.13 = f32[8,128,128,16]{2,3,1,0:T(8,128)} fusion(f32[8,16,128,128]{3,2,1,0:T(8,128)} %copy-done.1, bf16[16,16]{1,0:T(8,128)(2,1)S(1)} %copy-done), kind=kOutput, calls=%fused_computation.19 | convolution fusion | flops 402653184 | bytes 16777728 | tf_op jit(solution)/shard_map/szoxy,co->szcxy/dot_general | solution.py:148
  560.7 3.3 broadcast_multiply_fusion
  564.0 3.9 fusion.254
  567.8 6.0 reshape.232
  573.8 9.7 %fusion.108 = f32[8,16,1024]{2,0,1:T(8,128)S(1)} fusion(f32[16,1024,32]{2,1,0:T(8,128)} %reshape.232, s32[8]{0:T(128)S(1)} %iota_add_fusion), kind=kOutput, calls=%fused_computation.144 | convolution fusion | flops 50335232 | bytes 2621472 | tf_op jit(solution)/shard_map/scpk,zk->szcp/dot_general | solution.py:54
  583.6 7.2 %fusion.119 = f32[8,16,1024]{2,0,1:T(8,128)S(1)} fusion(f32[16,1024,32]{2,1,0:T(8,128)S(1)} %copy-done.3, s32[8]{0:T(128)S(1)} %iota_add_fusion), kind=kOutput, calls=%fused_computation.155 | convolution fusion | flops 50335232 | bytes 2621472 | tf_op jit(solution)/shard_map/scpk,zk->szcp/dot_general | solution.py:54
  590.8 4.7 reshape.233
  595.5 11.2 %convolution_add_fusion.2 = f32[8,16,1024]{2,0,1:T(8,128)} fusion(f32[8,16,1024]{2,0,1:T(8,128)S(1)} %fusion.108, f32[16,1024,32]{2,1,0:T(8,128)} %reshape.233, s32[8]{0:T(128)S(1)} %iota_add_fusion), kind=kOutput, calls=%fused_computation.76 | convolution fusion | flops 50466304 | bytes 3145760 | tf_op jit(solution)/shard_map/scpk,zk->szcp/dot_general | solution.py:54
  606.8 2.2 reshape.235
  608.9 4.9 fusion.29
  613.8 4.9 fusion.31
  618.7 9.6 %convolution_subtract_fusion.2 = f32[8,16,1024]{2,0,1:T(8,128)S(1)} fusion(f32[8,16,1024]{2,0,1:T(8,128)S(1)} %fusion.119, f32[16,1024,32]{2,1,0:T(8,128)} %reshape.233, s32[8]{0:T(128)S(1)} %iota_add_fusion), kind=kOutput, calls=%fused_computation.77 | convolution fusion | flops 50466304 | bytes 3145760 | tf_op jit(solution)/shard_map/scpk,zk->szcp/dot_general | solution.py:54
  629.0 5.3 subtract_bitcast_fusion
  634.3 3.6 add_bitcast_fusion
  637.9 18.4 %fusion.10 = bf16[1,8,16,128,128]{4,3,2,1,0:T(8,128)(2,1)} fusion(f32[8,128,128,16]{2,3,1,0:T(8,128)} %fusion.13, f32[1,8,16,128,32]{3,4,2,1,0:T(8,128)S(1)} %add_bitcast_fusion, f32[1,8,16,128,32]{3,4,2,1,0:T(8,128)S(1)} %subtract_bitcast_fusion, f32[128,32]{0,1:T(8,128)S(1)} %get-tuple-element.45, f32[128,32]{0,1:T(8,128)S(1)} %get-tuple-element.44), kind=kOutput, calls=%fused_computation.15 | convolution fusion | flops 1615863808 | bytes 16809984 | tf_op jit(solution)/shard_map/szcxb,yb->szcxy/dot_general | solution.py:73
  (50 shorter events, 6.2 us)
Async XLA Ops:
  7.2 150.6 %copy-start = (bf16[16,16]{1,0:T(8,128)(2,1)S(1)}, bf16[16,16]{1,0:T(8,128)(2,1)}, u32[]{:S(2)}) copy-start(bf16[16,16]{1,0:T(8,128)(2,1)} %param.7) | copy-start | bytes 1540
  7.2 148.5 %reduce-scatter.3.cloned.1.call-start = ((), (), s32[]{:S(2)}) async-start(), calls=%async_computation.2 | async-start | bytes 4325376 | tf_op jit(solution)/shard_map/reduce_scatter | solution.py:129
  59.8 7.6 %copy-start.6 = (f32[1,1,16,32768]{3,2,1,0:T(8,128)S(1)}, f32[1,1,16,32768]{3,2,1,0:T(8,128)}, u32[]{:S(2)}) copy-start(f32[1,1,16,32768]{3,2,1,0:T(8,128)} %stack_reshape.12) | copy-start | bytes 6291460
  71.5 85.1 %copy-start.8 = (bf16[2,16,16,1024]{3,2,1,0:T(8,128)(2,1)S(1)}, bf16[2,16,16,1024]{3,2,1,0:T(8,128)(2,1)}, u32[]{:S(2)}) copy-start(bf16[2,16,16,1024]{3,2,1,0:T(8,128)(2,1)} %param.6) | copy-start | bytes 3145732
  71.5 134.7 %all-gather.3.cloned.1.call-start = ((), (), s32[]{:S(2)}) async-start(), calls=%async_computation.3 | async-start | bytes 4325376 | tf_op jit(solution)/shard_map/all_gather | solution.py:131
  157.7 293.5 %reduce-scatter.5.cloned.1.call-start = ((), (), s32[]{:S(2)}) async-start(), calls=%async_computation.4 | async-start | bytes 4325376 | tf_op jit(solution)/shard_map/reduce_scatter | solution.py:142
  216.0 9.6 %copy-start.2 = (f32[16,1024,32]{2,1,0:T(8,128)S(1)}, f32[16,1024,32]{2,1,0:T(8,128)}, u32[]{:S(2)}) copy-start(f32[16,1024,32]{2,1,0:T(8,128)} %reshape.222) | copy-start | bytes 6291460
  270.8 5.3 copy-start.5
  276.1 3.6 copy-start.10
  304.1 9.5 %copy-start.1 = (f32[8,16,128,128]{3,2,1,0:T(8,128)}, f32[8,16,128,128]{3,2,1,0:T(8,128)S(1)}, u32[]{:S(2)}) copy-start(f32[8,16,128,128]{3,2,1,0:T(8,128)S(1)} %get-tuple-element.24) | copy-start | bytes 25165828
  360.1 7.1 %copy-start.7 = (f32[1,1,16,32768]{3,2,1,0:T(8,128)S(1)}, f32[1,1,16,32768]{3,2,1,0:T(8,128)}, u32[]{:S(2)}) copy-start(f32[1,1,16,32768]{3,2,1,0:T(8,128)} %stack_reshape.14) | copy-start | bytes 6291460
  371.4 80.8 %copy-start.9 = (bf16[2,16,16,1024]{3,2,1,0:T(8,128)(2,1)S(1)}, bf16[2,16,16,1024]{3,2,1,0:T(8,128)(2,1)}, u32[]{:S(2)}) copy-start(bf16[2,16,16,1024]{3,2,1,0:T(8,128)(2,1)} %param.6) | copy-start | bytes 3145732
  371.4 189.3 %all-reduce.2.cloned.1.call-start = ((), (), s32[]{:S(2)}) async-start(), calls=%async_computation.6 | async-start | bytes 4194304 | tf_op jit(solution)/shard_map/psum | solution.py:152
  454.7 109.3 %all-gather.5.cloned.1.call-start = ((), (), s32[]{:S(2)}) async-start(), calls=%async_computation.5 | async-start | bytes 4325376 | tf_op jit(solution)/shard_map/all_gather | solution.py:144
  573.8 9.8 %copy-start.3 = (f32[16,1024,32]{2,1,0:T(8,128)S(1)}, f32[16,1024,32]{2,1,0:T(8,128)}, u32[]{:S(2)}) copy-start(f32[16,1024,32]{2,1,0:T(8,128)} %reshape.232) | copy-start | bytes 6291460
  629.0 5.4 copy-start.4
Sparse Core Ops, SparseCore 0:
  71.6 84.0 reduce-scatter.2
  158.6 47.5 all-gather.2
  371.5 79.6 reduce-scatter.4
  454.9 59.8 all-reduce.1
  517.6 46.3 all-gather.4
where the time goes:
time: 672 us; the launch traced here: 663 us
  matrix products  261 us (39%)
  waiting for transfers between devices  204 us (30%)
  local copies, waits for them, and re-layouts  93.9 us (14%)
  blocking collectives  66.8 us (10%)
  other arithmetic  21.8 us (3%)
  between operations  14.3 us (2%)
    reduce_scatter x1, waiting for transfers between devices, shards(): lax.psum_scatter(partial_value, 'gz', scatter_dimension=3, tiled=True)  84.1 us
    reduce_scatter x1, waiting for transfers between devices, shards(): lax.psum_scatter(grad_partial, 'gz', scatter_dimension=3, tiled=True)  79.7 us
    dot_general x8, matrix products, expand(): return jnp.einsum('scpk,zk->szcp', values, table, precision=HIGHEST)  75.5 us
    psum x1, blocking collectives, shards(): point_total = lax.psum(point_term, ('dp', 'gz'))  66.8 us
    dot_general x2, matrix products, plane_inverse(): jnp.einsum('szcxb,yb->szcxy', joined, jnp.concatenate([cos_y, -sin_y], ax...  42.9 us
    all_gather x1, waiting for transfers between devices, shards(): whole = lax.all_gather(mixed, 'gz', axis=3, tiled=True)  40.5 us
    dot_general x8, matrix products, spread(): return jnp.einsum('szcab,xa->szcxb', values, table, precision=HIGHEST)  37.3 us
    another operation x12, local copies, waits for them, and re-layouts  34.1 us
  transfers between devices with their start and end apart: 5, of which 3 were waited for; matrix products, arithmetic and copies ran while one was open for 8% of the time, Pallas kernels for 0%

commit v1 on v0

v1 whole, which is shorter than its diff:
```python
import math

import jax
import jax.numpy as jnp
import ml_dtypes
import numpy as np
from jax import lax
from jax.experimental import pallas as pl
from jax.experimental.pallas import tpu as pltpu
from jax.sharding import PartitionSpec as P

M = 32
C = 16
ZL = 8
X = 128
Y = 128
Z = 256
GROUPS = 32
SAMPLES = 4
MODES = M * M * M
CELLS = SAMPLES * X * Y * Z
SCALE = 1.0 / math.sqrt(X * Y * Z * MODES)
BF = jnp.bfloat16
F32 = jnp.float32
VMEM_LIMIT = 60 * 1024 * 1024
K0 = math.sqrt(2.0 / math.pi)
K1 = K0 * 0.044715


def halves(table):
    high = table.astype(ml_dtypes.bfloat16)
    low = (table - high.astype(np.float64)).astype(ml_dtypes.bfloat16)
    return high, low


def wave(length, left, right):
    phase = np.outer(left, right) % length
    angle = phase * (2.0 * np.pi / length)
    return np.cos(angle), np.sin(angle)


def make_tables():
    modes = np.arange(M)
    ky = 4 * (modes % 8) + modes // 8
    tables = {}
    cos_x, sin_x = wave(X, modes, np.arange(X))
    high, low = halves(np.concatenate([cos_x, -sin_x]))
    zero = np.zeros_like(low)
    tables["xf"] = np.concatenate([high, low])
    tables["xg"] = np.concatenate(
        [np.concatenate([high, high], 1), np.concatenate([low, zero], 1)]
    )
    for name, scale in (("xi", SCALE), ("xj", 1.0)):
        high, low = halves(scale * np.concatenate([cos_x, -sin_x]).T)
        tables[name] = np.concatenate([high, high, low], 1)
    cos_y, sin_y = wave(Y, np.arange(Y), ky)
    forward = np.zeros((4, 2, Y, 2, 4, M))
    inverse = np.zeros((4, 2, 4, M, 2, Y))
    for k in range(4):
        forward[k, 0, :, 0, k] = cos_y
        forward[k, 1, :, 0, k] = sin_y
        forward[k, 0, :, 1, k] = -sin_y
        forward[k, 1, :, 1, k] = cos_y
        inverse[k, 0, k, :, 0] = cos_y.T
        inverse[k, 1, k, :, 0] = -sin_y.T
        inverse[k, 0, k, :, 1] = sin_y.T
        inverse[k, 1, k, :, 1] = cos_y.T
    tables["yf"] = np.stack(halves(forward.reshape(1024, 256)))
    tables["yi"] = np.stack(halves(inverse.reshape(1024, 256)))
    cos_z, sin_z = wave(Z, np.arange(Z), np.tile(modes, 4))
    tables["zf"] = np.stack(
        halves(
            np.concatenate(
                [np.concatenate([cos_z, -sin_z], 1), np.concatenate([sin_z, cos_z], 1)]
            )
        )
    )
    tables["zi"] = np.stack(halves(np.concatenate([cos_z, sin_z], 1)))
    return tables


TABLES = make_tables()


def dot(a, b):
    return lax.dot_general(a, b, (((1,), (0,)), ((), ())), preferred_element_type=F32)


def dot_nt(a, b):
    return lax.dot_general(a, b, (((1,), (1,)), ((), ())), preferred_element_type=F32)


def split(values):
    high = values.astype(BF)
    return high, (values - high.astype(F32)).astype(BF)


def rows_of_plane(section, lhs_high, lhs_low, first, k):
    for zz in range(2):
        lanes = slice(zz * Y, (zz + 1) * Y)
        row = jnp.concatenate([section[:M, lanes], section[M:, lanes]], axis=1)
        high, low = split(row)
        at = (slice((first + zz) * M, (first + zz + 1) * M), slice(k * 256, (k + 1) * 256))
        lhs_high[at] = high
        lhs_low[at] = low


def finish_forward(lhs_high, lhs_low, yf, out):
    high = lhs_high[...]
    total = dot(high, yf[0]) + dot(lhs_low[...], yf[0]) + dot(high, yf[1])
    flat = out.reshape(512, 128)
    for z in range(ZL):
        for part in range(2):
            flat[pl.ds(part * ZL + z, M, stride=16), :] = total[
                z * M : (z + 1) * M, part * 128 : (part + 1) * 128
            ]


def field_kernel(field, xf, yf, out, lhs_high, lhs_low):
    for zp in range(ZL // 2):
        for k in range(4):
            pair = jnp.concatenate([field[0, 2 * zp, k], field[0, 2 * zp + 1, k]], axis=1)
            both = dot(xf[...], pair)
            rows_of_plane(both[:64] + both[64:], lhs_high, lhs_low, 2 * zp, k)
    finish_forward(lhs_high, lhs_low, yf, out)


def depth_forward(planes, zf, rows):
    for group in range(4):
        for part in range(2):
            turned = planes[:, group, part * ZL : (part + 1) * ZL, :].reshape(Z, 128).T
            for k in range(4):
                for j in range(4):
                    rows[
                        j * 128 + (group * 4 + k) * 8 : j * 128 + (group * 4 + k + 1) * 8,
                        part * 256 : (part + 1) * 256,
                    ] = turned[k * 32 + j * 8 : k * 32 + j * 8 + 8]
    high, low = split(rows[...])
    wide = dot(high, zf[0]) + dot(low, zf[0]) + dot(high, zf[1])
    which = lax.broadcasted_iota(jnp.int32, (128, 256), 1) // 32 % 4
    total = wide[:128]
    for j in range(1, 4):
        total = jnp.where(which == j, wide[j * 128 : (j + 1) * 128], total)
    return total


def depth_inverse(spectrum, zi, out):
    lane = lax.broadcasted_iota(jnp.int32, (8, 128), 1) // 32
    for group in range(4):
        blocks = []
        for part in range(2):
            pieces = []
            for k in range(4):
                at = (group * 4 + k) * 8
                tile = spectrum[part, at : at + 8, :]
                pieces += [jnp.where(lane == j, tile, 0.0) for j in range(4)]
            blocks.append(jnp.concatenate(pieces, axis=0))
        real_in, imag_in = blocks
        right = jnp.concatenate(
            [
                jnp.concatenate([real_in, -imag_in], axis=1),
                jnp.concatenate([imag_in, real_in], axis=1),
            ],
            axis=0,
        )
        high, low = split(right)
        total = dot_nt(zi[0], high) + dot_nt(zi[0], low) + dot_nt(zi[1], high)
        for part in range(2):
            out[:, group, part * ZL : (part + 1) * ZL, :] = total[
                :, part * 128 : (part + 1) * 128
            ].reshape(GROUPS, ZL, 128)


def mix_kernel(planes, weight, zf, zi, spec_out, out, rows, mixed):
    spec = depth_forward(planes, zf, rows)
    spec_out[0] = spec[:, :128]
    spec_out[1] = spec[:, 128:]
    for g in range(8):
        lanes = slice(g * 128, (g + 1) * 128)
        real_out = jnp.zeros((C, 128), F32)
        imag_out = jnp.zeros((C, 128), F32)
        for c in range(C):
            real_in = spec_out[0, c * 8 + g : c * 8 + g + 1, :]
            imag_in = spec_out[1, c * 8 + g : c * 8 + g + 1, :]
            wr = weight[0, c, :, lanes].astype(F32)
            wi = weight[1, c, :, lanes].astype(F32)
            real_out += real_in * wr - imag_in * wi
            imag_out += real_in * wi + imag_in * wr
        mixed[0, pl.ds(g, C, stride=8), :] = real_out
        mixed[1, pl.ds(g, C, stride=8), :] = imag_out
    depth_inverse(mixed, zi, out)


def adjoint_kernel(planes, weight, zf, zi, spec_out, out, rows, mixed):
    spec = depth_forward(planes, zf, rows) * SCALE
    spec_out[0] = spec[:, :128]
    spec_out[1] = spec[:, 128:]
    for g in range(8):
        lanes = slice(g * 128, (g + 1) * 128)
        real_in = spec_out[0, pl.ds(g, C, stride=8), :]
        imag_in = spec_out[1, pl.ds(g, C, stride=8), :]
        for c in range(C):
            wr = weight[0, c, :, lanes].astype(F32)
            wi = weight[1, c, :, lanes].astype(F32)
            at = slice(c * 8 + g, c * 8 + g + 1)
            mixed[0, at, :] = jnp.sum(real_in * wr + imag_in * wi, axis=0, keepdims=True)
            mixed[1, at, :] = jnp.sum(imag_in * wr - real_in * wi, axis=0, keepdims=True)
    depth_inverse(mixed, zi, out)


def weight_grad_kernel(spec, grad, out):
    factor = math.sqrt(MODES / CELLS)
    for g in range(8):
        lanes = slice(g * 128, (g + 1) * 128)
        grads = [
            (
                grad[s, 0, pl.ds(g, C, stride=8), :] * factor,
                grad[s, 1, pl.ds(g, C, stride=8), :] * factor,
            )
            for s in range(SAMPLES)
        ]
        for c in range(C):
            real_out = jnp.zeros((C, 128), F32)
            imag_out = jnp.zeros((C, 128), F32)
            for s in range(SAMPLES):
                ur = spec[s, 0, c * 8 + g : c * 8 + g + 1, :]
                ui = spec[s, 1, c * 8 + g : c * 8 + g + 1, :]
                gr, gi = grads[s]
                real_out += ur * gr + ui * gi
                imag_out += ur * gi - ui * gr
            out[0, c, :, lanes] = real_out
            out[1, c, :, lanes] = imag_out


def plane_inverse(planes, yi, xi, store):
    flat = planes.reshape(512, 128)
    parts = [
        jnp.concatenate(
            [flat[pl.ds(part * ZL + z, M, stride=16), :] for part in range(2)], axis=1
        )
        for z in range(ZL)
    ]
    high, low = split(jnp.concatenate(parts, axis=0))
    for k in range(4):
        right = yi[0, k * 256 : (k + 1) * 256, :]
        middle = dot(high, right) + dot(low, right) + dot(high, yi[1, k * 256 : (k + 1) * 256, :])
        for zp in range(ZL // 2):
            first = middle[(2 * zp) * M : (2 * zp + 1) * M]
            second = middle[(2 * zp + 1) * M : (2 * zp + 2) * M]
            stacked = jnp.concatenate(
                [
                    jnp.concatenate([first[:, :Y], second[:, :Y]], axis=1),
                    jnp.concatenate([first[:, Y:], second[:, Y:]], axis=1),
                ],
                axis=0,
            )
            up, down = split(stacked)
            both = dot(xi[...], jnp.concatenate([up, down, up], axis=0))
            store(2 * zp, k, both[:, :Y])
            store(2 * zp + 1, k, both[:, Y:])


def cells_of(ref, zp, xb):
    pair = [
        ref[0, 2 * zp + zz, :, pl.ds(pl.multiple_of(xb * 16, 16), 16), :].reshape(C * 16, Y)
        for zz in range(2)
    ]
    return jnp.concatenate(pair, axis=1)


def output_kernel(
    planes, field, cot, pw, yi, xi, xg, yf,
    act_out, high_out, low_out, grad_planes, point_out,
    pre, lhs_high, lhs_low, point,
):
    def store(z, k, plane):
        pre[z, k] = plane

    plane_inverse(planes, yi, xi, store)
    point[...] = jnp.zeros_like(point)

    @pl.loop(0, X // 16)
    def _(xb):
        rows = pl.ds(pl.multiple_of(xb * 16, 16), 16)
        total = None
        for zp in range(ZL // 2):
            cells = cells_of(field, zp, xb)
            local = dot(pw[...], cells)
            grads = []
            for zz in range(2):
                z = 2 * zp + zz
                values = pre[z, :, rows, :].reshape(64, Y) + local[:, zz * Y : (zz + 1) * Y]
                square = values * values
                half = 0.5 + 0.5 * jnp.tanh(values * (K0 + K1 * square))
                act = values * half
                slope = half + values * (2.0 * K0 + 6.0 * K1 * square) * (half - half * half)
                grad = cot[0, z, :, rows, :].reshape(64, Y).astype(F32) * slope
                high, low = split(grad)
                act_out[0, z, :, rows, :] = act.astype(BF).reshape(4, 16, Y)
                high_out[0, z, :, rows, :] = high.reshape(4, 16, Y)
                low_out[0, z, :, rows, :] = low.reshape(4, 16, Y)
                grads.append(jnp.concatenate([high, low], axis=0))
            term = dot_nt(jnp.concatenate(grads, axis=1), cells)
            total = term if total is None else total + term
        point[...] += total

    both = point[0:64] + point[64:128]
    row = lax.broadcasted_iota(jnp.int32, (16, 256), 0)
    lane = lax.broadcasted_iota(jnp.int32, (16, 256), 1) % 16
    for k in range(4):
        kept = jnp.where(row == lane, both[k * 16 : (k + 1) * 16], 0.0)
        point_out[0, k : k + 1, :] = jnp.sum(kept, axis=0, keepdims=True)

    for zp in range(ZL // 2):
        for k in range(4):
            stacked = jnp.concatenate(
                [
                    jnp.concatenate([ref[0, 2 * zp, k], ref[0, 2 * zp + 1, k]], axis=1)
                    for ref in (high_out, low_out)
                ],
                axis=0,
            )
            both = dot(xg[...], stacked)
            rows_of_plane(both[:64] + both[64:], lhs_high, lhs_low, 2 * zp, k)
    finish_forward(lhs_high, lhs_low, yf, grad_planes)


def input_kernel(planes, high_in, low_in, pw, yi, xj, out, pre):
    def store(z, k, plane):
        pre[z, k] = plane

    plane_inverse(planes, yi, xj, store)

    @pl.loop(0, X // 16)
    def _(xb):
        rows = pl.ds(pl.multiple_of(xb * 16, 16), 16)
        for zp in range(ZL // 2):
            local = dot(pw[...], cells_of(high_in, zp, xb)) + dot(
                pw[...], cells_of(low_in, zp, xb)
            )
            for zz in range(2):
                z = 2 * zp + zz
                values = pre[z, :, rows, :].reshape(64, Y) + local[:, zz * Y : (zz + 1) * Y]
                out[0, z, :, rows, :] = values.astype(BF).reshape(4, 16, Y)


def whole(shape):
    return pl.BlockSpec(shape, lambda i: (0,) * len(shape))


GRID_BLOCK = pl.BlockSpec((1, ZL, 4, X, Y), lambda i: (0, 0, i, 0, 0))
GRID_FULL = whole((1, ZL, C, X, Y))
LANE_BLOCK = pl.BlockSpec((GROUPS, 1, 16, 128), lambda i: (0, i, 0, 0))
GRID_SHAPE = jax.ShapeDtypeStruct((1, ZL, C, X, Y), BF)
PLANES_SHAPE = jax.ShapeDtypeStruct((GROUPS, 4, 16, 128), F32)
SPEC_SHAPE = jax.ShapeDtypeStruct((2, 128, 128), F32)


def params():
    return pltpu.CompilerParams(vmem_limit_bytes=VMEM_LIMIT)


def table(name):
    return jnp.asarray(TABLES[name])


def field_forward(fields):
    return pl.pallas_call(
        field_kernel,
        grid=(4,),
        in_specs=[GRID_BLOCK, whole((128, 128)), whole((2, 1024, 256))],
        out_specs=LANE_BLOCK,
        out_shape=PLANES_SHAPE,
        scratch_shapes=[pltpu.VMEM((256, 1024), BF)] * 2,
        compiler_params=params(),
        name="field_forward",
    )(fields, table("xf"), table("yf"))


def mode_call(kernel, name, planes, weight):
    return pl.pallas_call(
        kernel,
        out_shape=(SPEC_SHAPE, PLANES_SHAPE),
        scratch_shapes=[pltpu.VMEM((512, 512), F32), pltpu.VMEM((2, 128, 128), F32)],
        compiler_params=params(),
        name=name,
    )(planes, weight, table("zf"), table("zi"))


def weight_grad(spec, grad):
    return pl.pallas_call(
        weight_grad_kernel,
        out_shape=jax.ShapeDtypeStruct((2, C, C, M * M), F32),
        compiler_params=params(),
        name="weight_grad",
    )(spec, grad)


def outputs(planes, fields, cotangent, pw):
    return pl.pallas_call(
        output_kernel,
        grid=(4,),
        in_specs=[
            LANE_BLOCK,
            GRID_FULL,
            GRID_BLOCK,
            pl.BlockSpec((64, 256), lambda i: (i, 0)),
            whole((2, 1024, 256)),
            whole((128, 192)),
            whole((128, 256)),
            whole((2, 1024, 256)),
        ],
        out_specs=(
            GRID_BLOCK,
            GRID_BLOCK,
            GRID_BLOCK,
            LANE_BLOCK,
            pl.BlockSpec((1, 4, 256), lambda i: (i, 0, 0)),
        ),
        out_shape=(
            GRID_SHAPE,
            GRID_SHAPE,
            GRID_SHAPE,
            PLANES_SHAPE,
            jax.ShapeDtypeStruct((4, 4, 256), F32),
        ),
        scratch_shapes=[
            pltpu.VMEM((ZL, 4, X, Y), F32),
            pltpu.VMEM((256, 1024), BF),
            pltpu.VMEM((256, 1024), BF),
            pltpu.VMEM((128, 256), F32),
        ],
        compiler_params=params(),
        name="outputs",
    )(planes, fields, cotangent, pw, table("yi"), table("xi"), table("xg"), table("yf"))


def input_grads(planes, high, low, pw):
    return pl.pallas_call(
        input_kernel,
        grid=(4,),
        in_specs=[
            LANE_BLOCK,
            GRID_FULL,
            GRID_FULL,
            pl.BlockSpec((64, 256), lambda i: (i, 0)),
            whole((2, 1024, 256)),
            whole((128, 192)),
        ],
        out_specs=GRID_BLOCK,
        out_shape=GRID_SHAPE,
        scratch_shapes=[pltpu.VMEM((ZL, 4, X, Y), F32)],
        compiler_params=params(),
        name="input_grads",
    )(planes, high, low, pw, table("yi"), table("xj"))


def exchange(planes):
    return lax.all_to_all(planes, "gz", 0, 0, tiled=True)


def shards(fields, cotangent, spectral_weight, pointwise_weight):
    eye = jnp.eye(16, dtype=BF)
    to_out = jnp.kron(pointwise_weight.T, eye)
    to_in = jnp.kron(pointwise_weight, eye)
    planes = exchange(field_forward(fields))
    spec, back = mode_call(mix_kernel, "mix", planes, spectral_weight)
    act, high, low, grad_planes, point = outputs(exchange(back), fields, cotangent, to_out)
    grad_spec, back = mode_call(adjoint_kernel, "adjoint", exchange(grad_planes), spectral_weight)
    grad_input = input_grads(exchange(back), high, low, to_in)
    spectral_grad = weight_grad(lax.all_gather(spec, "dp"), lax.all_gather(grad_spec, "dp"))
    point = point.reshape(C, C, 16).sum(-1).T
    pointwise_grad = lax.psum(point, ("dp", "gz")) * (1.0 / math.sqrt(CELLS))
    return act, grad_input, pointwise_grad, spectral_grad


def solution(mesh):
    placed = (
        P("dp", "gz", None, None, None),
        P("dp", "gz", None, None, None),
        P(None, None, None, "gz"),
        P(),
    )
    return jax.shard_map(
        shards,
        mesh=mesh,
        in_specs=placed,
        out_specs=(
            P("dp", "gz", None, None, None),
            P("dp", "gz", None, None, None),
            P(),
            P(None, None, None, "gz"),
        ),
        check_vma=False,
    )
```

time: 672 us -> 249 us (0.37); the launches traced: 663 us -> 247 us
  matrix products: 261 us -> 0 us
  waiting for transfers between devices: 204 us -> 14.9 us
  local copies, waits for them, and re-layouts: 93.9 us -> 6.21 us
  Pallas kernels: 0 us -> 78.2 us
  blocking collectives: 66.8 us -> 139 us
  other arithmetic: 21.8 us -> 0.32 us
  between operations: 14.3 us -> 0.7 us
  starting transfers between devices: 0.38 us -> 7.96 us
    dot_general x33 -> x0, matrix products: 261 us -> none  [the longest x8 75.5 us: expand(): return jnp.einsum('scpk,zk->szcp', values, table, precision=HIGHEST)]
    reduce_scatter x2 -> x0, waiting for transfers between devices: 164 us -> none  [the longest x1 84.1 us: shards(): lax.psum_scatter(partial_value, 'gz', scatter_dimension=3, tiled=True)]
    pallas_call x0 -> x6, Pallas kernels: none -> 78.2 us  [the longest x1 36.1 us: outputs(): pl.pallas_call(output_kernel, grid=(4,), in_specs=[LANE_BLOCK, GRID_FULL,...]
    another operation x16 -> x0, local copies, waits for them, and re-layouts: 62.8 us -> none
    all_to_all x0 -> x2, blocking collectives: none -> 48.3 us  [exchange(): return lax.all_to_all(planes, 'gz', 0, 0, tiled=True)]
    all_gather x2 -> x0, waiting for transfers between devices: 40.5 us -> none  [the longest x1 40.5 us: shards(): whole = lax.all_gather(mixed, 'gz', axis=3, tiled=True)]
    all_gather x0 -> x2, blocking collectives: none -> 23.3 us  [the longest x1 11.6 us: shards(): lax.all_gather(spec, 'dp')]
    all_to_all x0 -> x2, waiting for transfers between devices: none -> 14.9 us  [exchange(): return lax.all_to_all(planes, 'gz', 0, 0, tiled=True)]
  transfers between devices with their start and end apart: 5 -> 2, of which waited for: 3 -> 1; matrix products, arithmetic and copies ran while one was open for 8% -> 2% of each run, Pallas kernels for 0% -> 1%
where the time goes in v1:
time: 249 us; the launch traced here: 247 us
  blocking collectives  139 us (56%)
  Pallas kernels  78.2 us (31%)
  waiting for transfers between devices  14.9 us (6%)
  starting transfers between devices  7.96 us (3%)
  local copies, waits for them, and re-layouts  6.21 us (2%)
    psum x1, blocking collectives, shards(): pointwise_grad = lax.psum(point, ('dp', 'gz')) * (1.0 / math.sqrt(CELLS))  67 us
    all_to_all x2, blocking collectives, exchange(): return lax.all_to_all(planes, 'gz', 0, 0, tiled=True)  48.3 us
    pallas_call x1, Pallas kernels, outputs(): pl.pallas_call(output_kernel, grid=(4,), in_specs=[LANE_BLOCK, GRID_FULL,...  36.1 us
    pallas_call x1, Pallas kernels, input_grads(): pl.pallas_call(input_kernel, grid=(4,), in_specs=[LANE_BLOCK, GRID_FULL,...  21.6 us
    all_to_all x2, waiting for transfers between devices, exchange(): return lax.all_to_all(planes, 'gz', 0, 0, tiled=True)  14.9 us
    all_gather x1, blocking collectives, shards(): lax.all_gather(spec, 'dp')  11.6 us
    all_gather x1, blocking collectives, shards(): lax.all_gather(grad_spec, 'dp')  11.6 us
    pallas_call x2, Pallas kernels, mode_call(): pl.pallas_call(kernel, out_shape=(SPEC_SHAPE, PLANES_SHAPE), scratch_shap...  10.4 us
  transfers between devices with their start and end apart: 2, of which 1 were waited for; matrix products, arithmetic and copies ran while one was open for 2% of the time, Pallas kernels for 1%

profile of v1, /device:TPU:1, one launch (start us, length us, event | category | flops | bytes accessed | tf_op | source)
XLA Modules:
  0.0 246.9 jit_solution(1590219689262730365)
XLA Ops:
  0.6 6.6 %field_forward.1 = f32[32,4,16,128]{3,2,1,0:T(8,128)} custom-call(bf16[1,8,16,128,128]{4,3,2,1,0:T(8,128)(2,1)} %field.3, bf16[128,128]{1,0:T(8,128)(2,1)} %constant.20.clone.xf, bf16[2,1024,256]{2,1,0:T(8,128)(2,1)} %constant.21.clone.yf), custom_call_target="tpu_custom_call" | custom-call | tf_op jit(solution)/shard_map/field_forward/pallas_call | solution.py:368
  7.2 0.0 copy-start.4
  7.2 26.7 %all_to_all.20.planes = f32[32,4,16,128]{3,2,1,0:T(8,128)} all-to-all(f32[32,4,16,128]{3,2,1,0:T(8,128)} %field_forward.1), channel_id=1, replica_groups=mesh['dp'=4,'gz'=32] {'gz'}, dimensions={0} | all-to-all | bytes 2097152 | tf_op jit(solution)/shard_map/all_to_all | solution.py:459
  33.9 5.2 %mix.1 = (f32[2,128,128]{2,1,0:T(8,128)}, f32[32,4,16,128]{3,2,1,0:T(8,128)}) custom-call(f32[32,4,16,128]{3,2,1,0:T(8,128)} %all_to_all.20.planes, bf16[2,16,16,1024]{3,2,1,0:T(8,128)(2,1)} %weight.3, bf16[2,512,256]{2,1,0:T(8,128)(2,1)} %constant.22.clone.zf, bf16[2,256,256]{2,1,0:T(8,128)(2,1)} %constant.23.clone.zi), custom_call_target="tpu_custom_call" | custom-call | tf_op jit(solution)/shard_map/mix/pallas_call | solution.py:381
  39.2 3.9 %all-to-all-start.1 = ((f32[32,4,16,128]{3,2,1,0:T(8,128)}), f32[32,4,16,128]{3,2,1,0:T(8,128)S(1)}, u32[]{:S(2)}, u32[]{:S(2)}) async-start(f32[32,4,16,128]{3,2,1,0:T(8,128)} %get-tuple-element.13), calls=%async_computation.1 | async-start | bytes 2097152 | tf_op jit(solution)/shard_map/all_to_all | solution.py:459
  43.1 0.0 copy-done.4
  43.1 0.1 copy.17
  43.2 0.2 broadcast_multiply_fusion
  43.4 1.7 mul.50.pw
  45.1 14.9 %all-to-all-done.1.planes = f32[32,4,16,128]{3,2,1,0:T(8,128)S(1)} async-done(((f32[32,4,16,128]{3,2,1,0:T(8,128)}), f32[32,4,16,128]{3,2,1,0:T(8,128)S(1)}, u32[]{:S(2)}, u32[]{:S(2)}) %all-to-all-start.1) | async-done | bytes 1048608 | tf_op jit(solution)/shard_map/all_to_all | solution.py:459
  60.0 0.0 copy-start.1
  60.0 1.0 copy-done.1
  61.0 36.1 %outputs.1 = (bf16[1,8,16,128,128]{4,3,2,1,0:T(8,128)(2,1)}, bf16[1,8,16,128,128]{4,3,2,1,0:T(8,128)(2,1)}, bf16[1,8,16,128,128]{4,3,2,1,0:T(8,128)(2,1)}, f32[32,4,16,128]{3,2,1,0:T(8,128)}, f32[4,4,256]{2,1,0:T(4,128)}) custom-call(f32[32,4,16,128]{3,2,1,0:T(8,128)} %copy-done.1, bf16[1,8,16,128,128]{4,3,2,1,0:T(8,128)(2,1)} %field.3, ...), custom_call_target="tpu_custom_call" | custom-call | tf_op jit(solution)/shard_map/outputs/pallas_call | solution.py:400
  97.1 0.0 copy-start.2
  97.1 0.0 copy-start.5
  97.1 21.5 %all_to_all.21.planes = f32[32,4,16,128]{3,2,1,0:T(8,128)} all-to-all(f32[32,4,16,128]{3,2,1,0:T(8,128)} %get-tuple-element.15), channel_id=1, replica_groups=mesh['dp'=4,'gz'=32] {'gz'}, dimensions={0} | all-to-all | bytes 2097152 | tf_op jit(solution)/shard_map/all_to_all | solution.py:459
  118.6 5.1 %adjoint.1 = (f32[2,128,128]{2,1,0:T(8,128)}, f32[32,4,16,128]{3,2,1,0:T(8,128)}) custom-call(f32[32,4,16,128]{3,2,1,0:T(8,128)} %all_to_all.21.planes, bf16[2,16,16,1024]{3,2,1,0:T(8,128)(2,1)} %weight.3, bf16[2,512,256]{2,1,0:T(8,128)(2,1)} %constant.22.clone.zf, bf16[2,256,256]{2,1,0:T(8,128)(2,1)} %constant.23.clone.zi), custom_call_target="tpu_custom_call" | custom-call | tf_op jit(solution)/shard_map/adjoint/pallas_call | solution.py:381
  123.8 0.0 copy-start.3
  123.8 4.0 %all-to-all-start.3 = ((f32[32,4,16,128]{3,2,1,0:T(8,128)}), f32[32,4,16,128]{3,2,1,0:T(8,128)S(1)}, u32[]{:S(2)}, u32[]{:S(2)}) async-start(f32[32,4,16,128]{3,2,1,0:T(8,128)} %get-tuple-element.16), calls=%async_computation.3 | async-start | bytes 2097152 | tf_op jit(solution)/shard_map/all_to_all | solution.py:459
  127.8 1.6 mul.53.pw
  129.5 0.0 copy-done.2
  129.5 11.6 %all-gather = f32[8,128,128]{2,1,0:T(8,128)} all-gather(f32[2,128,128]{2,1,0:T(8,128)S(1)} %copy-done.2), channel_id=2, replica_groups=mesh['dp'=4,'gz'=32] {'dp'}, dimensions={0}, use_global_device_ids=true | all-gather | bytes 655360 | tf_op jit(solution)/shard_map/all_gather | solution.py:471
  141.1 0.0 copy-done.5
  141.1 0.1 reshape.30
  141.2 0.1 reduce_sum.9
  141.3 67.0 %psum.7 = f32[16,16]{0,1:T(8,128)S(1)} all-reduce(f32[16,16]{0,1:T(8,128)S(1)} %bitcast.10), channel_id=1, replica_groups=mesh['dp'=4,'gz'=32] {'dp','gz'}, use_global_device_ids=true, to_apply=%region_1.2 | all-reduce | flops 256 | bytes 2048 | tf_op jit(solution)/shard_map/psum | solution.py:473
  208.3 0.7 copy.18
  209.0 0.0 copy-done.3
  209.0 11.6 %all-gather.1 = f32[8,128,128]{2,1,0:T(8,128)} all-gather(f32[2,128,128]{2,1,0:T(8,128)S(1)} %copy-done.3), channel_id=3, replica_groups=mesh['dp'=4,'gz'=32] {'dp'}, dimensions={0}, use_global_device_ids=true | all-gather | bytes 655360 | tf_op jit(solution)/shard_map/all_gather | solution.py:471
  220.6 3.6 %weight_grad.1 = f32[2,16,16,1024]{3,2,1,0:T(8,128)} custom-call(f32[4,2,128,128]{3,2,1,0:T(8,128)} %bitcast.8, f32[4,2,128,128]{3,2,1,0:T(8,128)} %bitcast.9), custom_call_target="tpu_custom_call" | custom-call | tf_op jit(solution)/shard_map/weight_grad/pallas_call | solution.py:391
  224.2 0.0 all-to-all-done.3.planes
  224.2 0.0 copy-start
  224.2 1.1 copy-done
  225.3 21.6 %input_grads.1 = bf16[1,8,16,128,128]{4,3,2,1,0:T(8,128)(2,1)} custom-call(f32[32,4,16,128]{3,2,1,0:T(8,128)} %copy-done, bf16[1,8,16,128,128]{4,3,2,1,0:T(8,128)(2,1)} %get-tuple-element.17.high_in, bf16[1,8,16,128,128]{4,3,2,1,0:T(8,128)(2,1)} %get-tuple-element.18.low_in, bf16[256,256]{1,0:T(8,128)(2,1)} %mul.53.pw, ...), custom_call_target="tpu_custom_call" | custom-call | tf_op jit(solution)/shard_map/input_grads/pallas_call | solution.py:439
  (2 shorter events, 0.0 us)
Async XLA Ops:
  7.2 35.9 %copy-start.4 = (bf16[16,16]{1,0:T(8,128)(2,1)S(1)}, bf16[16,16]{1,0:T(8,128)(2,1)}, u32[]{:S(2)}) copy-start(bf16[16,16]{1,0:T(8,128)(2,1)} %param.15) | copy-start | bytes 1540
  39.2 20.8 %all-to-all-start.1 = ((f32[32,4,16,128]{3,2,1,0:T(8,128)}), f32[32,4,16,128]{3,2,1,0:T(8,128)S(1)}, u32[]{:S(2)}, u32[]{:S(2)}) async-start(f32[32,4,16,128]{3,2,1,0:T(8,128)} %get-tuple-element.13), calls=%async_computation.1 | async-start | bytes 2097152 | tf_op jit(solution)/shard_map/all_to_all | solution.py:459
  60.0 1.0 copy-start.1
  97.1 32.4 %copy-start.2 = (f32[2,128,128]{2,1,0:T(8,128)S(1)}, f32[2,128,128]{2,1,0:T(8,128)}, u32[]{:S(2)}) copy-start(f32[2,128,128]{2,1,0:T(8,128)} %get-tuple-element.20) | copy-start | bytes 393220
  97.1 44.0 %copy-start.5 = (f32[4,4,256]{2,1,0:T(4,128)S(1)}, f32[4,4,256]{2,1,0:T(4,128)}, u32[]{:S(2)}) copy-start(f32[4,4,256]{2,1,0:T(4,128)} %get-tuple-element.19) | copy-start | bytes 49156
  123.8 85.2 %copy-start.3 = (f32[2,128,128]{2,1,0:T(8,128)S(1)}, f32[2,128,128]{2,1,0:T(8,128)}, u32[]{:S(2)}) copy-start(f32[2,128,128]{2,1,0:T(8,128)} %get-tuple-element.21) | copy-start | bytes 393220
  123.8 100.5 %all-to-all-start.3 = ((f32[32,4,16,128]{3,2,1,0:T(8,128)}), f32[32,4,16,128]{3,2,1,0:T(8,128)S(1)}, u32[]{:S(2)}, u32[]{:S(2)}) async-start(f32[32,4,16,128]{3,2,1,0:T(8,128)} %get-tuple-element.16), calls=%async_computation.3 | async-start | bytes 2097152 | tf_op jit(solution)/shard_map/all_to_all | solution.py:459
  224.2 1.1 copy-start

commit v2 on v0

v2 whole, which is shorter than its diff:
```python
import math

import jax
import jax.numpy as jnp
import ml_dtypes
import numpy as np
from jax import lax
from jax.experimental import pallas as pl
from jax.experimental.pallas import tpu as pltpu
from jax.sharding import PartitionSpec as P

M = 32
C = 16
ZL = 8
X = 128
Y = 128
Z = 256
GROUPS = 32
SAMPLES = 4
MODES = M * M * M
CELLS = SAMPLES * X * Y * Z
SCALE = 1.0 / math.sqrt(X * Y * Z * MODES)
BF = jnp.bfloat16
F32 = jnp.float32
VMEM_LIMIT = 62 * 1024 * 1024
K0 = math.sqrt(2.0 / math.pi)
K1 = K0 * 0.044715
MESH = pl.DeviceIdType.MESH


def halves(table):
    high = table.astype(ml_dtypes.bfloat16)
    low = (table - high.astype(np.float64)).astype(ml_dtypes.bfloat16)
    return high, low


def wave(length, left, right):
    phase = np.outer(left, right) % length
    angle = phase * (2.0 * np.pi / length)
    return np.cos(angle), np.sin(angle)


def make_tables():
    modes = np.arange(M)
    ky = 4 * (modes % 8) + modes // 8
    tables = {}
    cos_y, sin_y = wave(Y, ky, np.arange(Y))
    high, low = halves(np.concatenate([cos_y, -sin_y]))
    tables["yf"] = np.concatenate([high, low])
    tables["yg"] = np.concatenate(
        [np.concatenate([high, high], 1), np.concatenate([low, np.zeros_like(low)], 1)]
    )
    cos_x, sin_x = wave(X, modes, np.arange(X))
    high, low = halves(
        np.concatenate(
            [np.concatenate([cos_x, sin_x], 1), np.concatenate([-sin_x, cos_x], 1)]
        )
    )
    tables["xf"] = np.concatenate([high, low])
    high, low = halves(
        np.concatenate(
            [np.concatenate([cos_y, sin_y], 1), np.concatenate([-sin_y, cos_y], 1)]
        )
    )
    zero = np.zeros_like(low)
    tables["yi"] = np.stack(
        [np.concatenate([high, high, low, zero]), np.concatenate([high, high, zero, low])]
    )
    for name, scale in (("xi", SCALE), ("xj", 1.0)):
        high, low = halves(scale * np.concatenate([cos_x, -sin_x]).T)
        tables[name] = np.concatenate([high, high, low], 1)
    cos_z, sin_z = wave(Z, np.arange(Z), np.tile(modes, 4))
    tables["zf"] = np.stack(
        halves(
            np.concatenate(
                [np.concatenate([cos_z, -sin_z], 1), np.concatenate([sin_z, cos_z], 1)]
            )
        )
    )
    tables["zi"] = np.stack(halves(np.concatenate([cos_z, sin_z], 1)))
    return tables


TABLES = make_tables()
NAMES = ("yf", "yg", "xf", "yi", "xi", "xj", "zf", "zi")


def dot(a, b):
    return lax.dot_general(a, b, (((1,), (0,)), ((), ())), preferred_element_type=F32)


def dot_nt(a, b, precision=None):
    return lax.dot_general(
        a, b, (((1,), (1,)), ((), ())), preferred_element_type=F32, precision=precision
    )


def split(values):
    high = values.astype(BF)
    return high, (values - high.astype(F32)).astype(BF)


def side(arrays):
    return jnp.concatenate(arrays, axis=1)


def stack(arrays):
    return jnp.concatenate(arrays, axis=0)


def forward_x(sections, xf, out, group, zp):
    rows = []
    for zz in range(2):
        at = slice(zz * X, (zz + 1) * X)
        rows += [side([section[:M, at], section[M:, at]]) for section in sections]
    high, low = split(stack(rows))
    wide = dot_nt(xf[...], high)
    total = wide[:64] + wide[64:] + dot_nt(xf[0:64, :], low)
    flat = out.reshape(GROUPS * 64, 128)
    for zz in range(2):
        for part in range(2):
            first = group * 16 + part * ZL + 2 * zp + zz
            flat[pl.ds(first, M, stride=64), :] = total[
                part * M : (part + 1) * M, zz * 128 : (zz + 1) * 128
            ]


def field_forward(field, yf, xf, out, group):
    @pl.loop(0, ZL // 2)
    def _(zp):
        sections = []
        for k in range(4):
            c = group * 4 + k
            both = dot_nt(yf[...], stack([field[2 * zp, c], field[2 * zp + 1, c]]))
            sections.append(both[:64] + both[64:])
        forward_x(sections, xf, out, group, zp)


def depth_rows(planes, rows, group):
    for part in range(2):
        turned = planes[:, group, part * ZL : (part + 1) * ZL, :].reshape(Z, 128).T
        for k in range(4):
            for j in range(4):
                at = pl.multiple_of(j * 128 + (group * 4 + k) * 8, 8)
                rows[pl.ds(at, 8), part * 256 : (part + 1) * 256] = turned[
                    k * 32 + j * 8 : k * 32 + j * 8 + 8
                ]


def depth_forward(rows, zf):
    which = lax.broadcasted_iota(jnp.int32, (128, 256), 1) // 32 % 4
    total = None
    for j in range(4):
        high, low = split(rows[j * 128 : (j + 1) * 128, :])
        wide = dot(high, zf[0]) + dot(low, zf[0]) + dot(high, zf[1])
        total = wide if total is None else jnp.where(which == j, wide, total)
    return total


def depth_inverse(spectrum, zi, out, group):
    lane = lax.broadcasted_iota(jnp.int32, (8, 128), 1) // 32
    right = []
    for k in range(4):
        at = pl.ds(pl.multiple_of((group * 4 + k) * 8, 8), 8)
        real_in = spectrum[0, at, :]
        imag_in = spectrum[1, at, :]
        real_in = stack([jnp.where(lane == j, real_in, 0.0) for j in range(4)])
        imag_in = stack([jnp.where(lane == j, imag_in, 0.0) for j in range(4)])
        right += [side([real_in, -imag_in]), side([imag_in, real_in])]
    high, low = split(stack(right))
    total = dot_nt(zi[0], high) + dot_nt(zi[0], low) + dot_nt(zi[1], high)
    for pair in range(2):
        out[:, group, pair * ZL : (pair + 1) * ZL, :] = total[
            :, pair * 128 : (pair + 1) * 128
        ].reshape(GROUPS, ZL, 128)


def mix(spec, weight, mixed):
    @pl.loop(0, 8)
    def _(g):
        lanes = pl.ds(pl.multiple_of(g * 128, 128), 128)
        real_out = jnp.zeros((C, 128), F32)
        imag_out = jnp.zeros((C, 128), F32)
        for c in range(C):
            real_in = spec[0, pl.ds(c * 8 + g, 1), :]
            imag_in = spec[1, pl.ds(c * 8 + g, 1), :]
            wr = weight[0, c, :, lanes].astype(F32)
            wi = weight[1, c, :, lanes].astype(F32)
            real_out += real_in * wr - imag_in * wi
            imag_out += real_in * wi + imag_in * wr
        mixed[0, pl.ds(g, C, stride=8), :] = real_out
        mixed[1, pl.ds(g, C, stride=8), :] = imag_out


def mix_adjoint(spec, weight, mixed):
    @pl.loop(0, 8)
    def _(g):
        lanes = pl.ds(pl.multiple_of(g * 128, 128), 128)
        real_in = spec[0, pl.ds(g, C, stride=8), :]
        imag_in = spec[1, pl.ds(g, C, stride=8), :]
        for c in range(C):
            wr = weight[0, c, :, lanes].astype(F32)
            wi = weight[1, c, :, lanes].astype(F32)
            at = pl.ds(c * 8 + g, 1)
            mixed[0, at, :] = jnp.sum(real_in * wr + imag_in * wi, axis=0, keepdims=True)
            mixed[1, at, :] = jnp.sum(imag_in * wr - real_in * wi, axis=0, keepdims=True)


def weight_grad(spec, grad, out):
    factor = math.sqrt(MODES / CELLS)

    @pl.loop(0, 8)
    def _(g):
        lanes = pl.ds(pl.multiple_of(g * 128, 128), 128)
        grads = [
            [grad[s, part, pl.ds(g, C, stride=8), :] * factor for part in range(2)]
            for s in range(SAMPLES)
        ]
        for c in range(C):
            real_out = jnp.zeros((C, 128), F32)
            imag_out = jnp.zeros((C, 128), F32)
            for s in range(SAMPLES):
                ur = spec[s, 0, pl.ds(c * 8 + g, 1), :]
                ui = spec[s, 1, pl.ds(c * 8 + g, 1), :]
                gr, gi = grads[s]
                real_out += ur * gr + ui * gi
                imag_out += ur * gi - ui * gr
            out[0, c, :, lanes] = real_out
            out[1, c, :, lanes] = imag_out


def inverse_y(planes, yi, middle, group):
    flat = planes.reshape(GROUPS * 64, 128)
    lane = lax.broadcasted_iota(jnp.int32, (256, 128), 1)
    for pair in range(2):
        values = stack(
            [flat[pl.ds(group * 16 + pair * ZL + z, M, stride=64), :] for z in range(ZL)]
        )
        high = values.astype(BF)
        wide = high.astype(F32)
        turned = pltpu.roll(values - wide, 64, 1)
        even = jnp.where(lane < 64, wide, turned).astype(BF)
        odd = jnp.where(lane < 64, turned, wide).astype(BF)
        middle[2 * pair] = dot(side([even, high]), yi[0])
        middle[2 * pair + 1] = dot(side([odd, high]), yi[1])


def inverse_x(middle, table, zp, k):
    first = middle[k, pl.ds(pl.multiple_of(2 * zp * M, M), M), :]
    second = middle[k, pl.ds(pl.multiple_of((2 * zp + 1) * M, M), M), :]
    high, low = split(
        stack([side([first[:, :Y], second[:, :Y]]), side([first[:, Y:], second[:, Y:]])])
    )
    return dot(table[...], stack([high, low, high]))


def cells_of(ref, zp, rows):
    return side([ref[2 * zp + zz, :, rows, :].reshape(C * 16, Y) for zz in range(2)])


def spread(ref, lefts, local):
    @pl.loop(0, X // 16)
    def _(xb):
        rows = pl.ds(pl.multiple_of(xb * 16, 16), 16)
        for zp in range(ZL // 2):
            total = None
            for source in lefts:
                term = dot(ref[...], cells_of(source, zp, rows))
                total = term if total is None else total + term
            for zz in range(2):
                local[2 * zp + zz, :, rows, :] = total[:, zz * Y : (zz + 1) * Y].reshape(
                    C, 16, Y
                )


def step_kernel(*refs):
    fields, cotangent, weights, pointwise = refs[:4]
    sources = dict(zip(NAMES, refs[4 : 4 + len(NAMES)]))
    refs = refs[4 + len(NAMES) :]
    act_out, grad_out, point_out, spec_grad_out = refs[:4]
    refs = refs[4:]
    tables = dict(zip(NAMES, refs[: len(NAMES)]))
    refs = refs[len(NAMES) :]
    (
        field, cot, weight, act, grad_in, high_g, low_g, local,
        send_a, recv_a, send_b, recv_b, send_c, recv_c, send_d, recv_d,
        specs, grads, mixed, rows_ref, middle, spread_out, spread_in, point_acc, spec_grad,
        point_z, point_y, point_x,
        load_sem, store_sem, send_sem, recv_sem, small_send, small_recv,
    ) = refs
    me = lax.axis_index("gz")
    dp = lax.axis_index("dp")

    barrier = pltpu.get_barrier_semaphore()

    @pl.loop(1, GROUPS)
    def _(k):
        pl.semaphore_signal(
            barrier, inc=1, device_id=(dp, lax.rem(me + k, GROUPS)), device_id_type=MESH
        )

    for k in range(1, SAMPLES):
        pl.semaphore_signal(
            barrier, inc=1, device_id=(lax.rem(dp + k, SAMPLES), me), device_id_type=MESH
        )

    def channels(group):
        return pl.ds(group * 4, 4)

    def field_load(group):
        return pltpu.make_async_copy(
            fields.at[0, :, channels(group)], field.at[:, channels(group)], load_sem.at[group]
        )

    def cot_load(group):
        return pltpu.make_async_copy(
            cotangent.at[0, :, channels(group)], cot.at[:, channels(group)], load_sem.at[4 + group]
        )

    def table_load(name):
        return pltpu.make_async_copy(
            sources[name], tables[name], load_sem.at[8 + NAMES.index(name)]
        )

    weight_load = pltpu.make_async_copy(weights, weight, load_sem.at[16])
    for name in ("yf", "xf"):
        table_load(name).start()
    for group in range(4):
        field_load(group).start()
    for name in NAMES:
        if name not in ("yf", "xf"):
            table_load(name).start()
    weight_load.start()
    for group in range(4):
        cot_load(group).start()

    def send(index, group, source, target):
        @pl.loop(1, GROUPS)
        def _(k):
            peer = lax.rem(me + k, GROUPS)
            pltpu.make_async_remote_copy(
                src_ref=source.at[peer, group],
                dst_ref=target.at[me, group],
                send_sem=send_sem.at[index, group],
                recv_sem=recv_sem.at[index, group],
                device_id=(dp, peer),
                device_id_type=MESH,
            ).start()

        target[me, group] = source[me, group]

    def wait_planes(sem, index, group, buffer):
        part = buffer.at[pl.ds(0, GROUPS - 1), group]
        pltpu.make_async_copy(part, part, sem.at[index, group]).wait()

    def small(index, buffer, slot, count, place):
        for k in range(1, count):
            pltpu.make_async_remote_copy(
                src_ref=buffer.at[slot],
                dst_ref=buffer.at[slot],
                send_sem=small_send.at[index],
                recv_sem=small_recv.at[index],
                device_id=place(k),
                device_id_type=MESH,
            ).start()

    def small_wait(sem, index, buffer, count):
        part = buffer.at[pl.ds(0, count - 1)]
        pltpu.make_async_copy(part, part, sem.at[index]).wait()

    def along_dp(k):
        return lax.rem(dp + k, SAMPLES), me

    def along_z(k):
        return dp, me // 8 * 8 + lax.rem(me + k, 8)

    def along_y(k):
        return dp, lax.rem(me + 8 * k, GROUPS)

    for name in ("yf", "xf"):
        table_load(name).wait()

    field_load(0).wait()
    field_forward(field, tables["yf"], tables["xf"], send_a, 0)
    pl.semaphore_wait(barrier, GROUPS - 1 + SAMPLES - 1)
    send(0, 0, send_a, recv_a)

    @pl.loop(1, 4)
    def _(group):
        field_load(group).wait()
        field_forward(field, tables["yf"], tables["xf"], send_a, group)
        send(0, group, send_a, recv_a)

    place = lax.broadcasted_iota(jnp.int32, (256, C), 0) // 16
    one_hot = (place == lax.broadcasted_iota(jnp.int32, (256, C), 1)).astype(F32).astype(BF)
    same = (
        lax.broadcasted_iota(jnp.int32, (256, 256), 0) % 16
        == lax.broadcasted_iota(jnp.int32, (256, 256), 1) % 16
    )
    for left, target in (
        (dot_nt(one_hot, pointwise[...]), spread_out),
        (dot(one_hot, pointwise[...]), spread_in),
    ):
        target[...] = jnp.where(same, dot_nt(left.astype(BF), one_hot), 0.0).astype(BF)
    spread(spread_out, (field,), local)
    for name in NAMES:
        if name not in ("yf", "xf"):
            table_load(name).wait()
    weight_load.wait()

    @pl.loop(0, 4)
    def _(group):
        wait_planes(recv_sem, 0, group, recv_a)
        depth_rows(recv_a, rows_ref, group)

    spec = depth_forward(rows_ref, tables["zf"])
    specs[dp, 0] = spec[:, :128]
    specs[dp, 1] = spec[:, 128:]
    mix(specs.at[dp], weight, mixed)

    @pl.loop(0, 4)
    def _(group):
        depth_inverse(mixed, tables["zi"], send_b, group)
        send(1, group, send_b, recv_b)

    small(0, specs, dp, SAMPLES, along_dp)

    @pl.loop(0, 4)
    def _(group):
        wait_planes(recv_sem, 1, group, recv_b)
        inverse_y(recv_b, tables["yi"], middle, group)
        cot_load(group).wait()

        @pl.loop(0, ZL // 2)
        def _(zp):
            sections = []
            for k in range(4):
                o = group * 4 + k
                both = inverse_x(middle, tables["xi"], zp, k)
                right = []
                for zz in range(2):
                    z = 2 * zp + zz
                    values = both[:, zz * Y : (zz + 1) * Y] + local[z, o]
                    square = values * values
                    half = 0.5 + 0.5 * jnp.tanh(values * (K0 + K1 * square))
                    act[z, o] = (values * half).astype(BF)
                    slope = half + values * (2.0 * K0 + 6.0 * K1 * square) * (half - half * half)
                    high, low = split(cot[z, o].astype(F32) * slope)
                    high_g[z, o] = high
                    low_g[z, o] = low
                    right.append(side([high, low]))
                wide = dot_nt(tables["yg"][...], stack(right))
                sections.append(wide[:64] + wide[64:])
            forward_x(sections, tables["xf"], send_c, group, zp)

        send(2, group, send_c, recv_c)
        pltpu.make_async_copy(
            act.at[:, channels(group)], act_out.at[0, :, channels(group)], store_sem.at[0]
        ).start()

    point_acc[...] = jnp.zeros_like(point_acc)

    @pl.loop(0, X // 16)
    def _(xb):
        rows = pl.ds(pl.multiple_of(xb * 16, 16), 16)
        total = None
        for zp in range(ZL // 2):
            cells = cells_of(field, zp, rows)
            term = dot_nt(cells_of(high_g, zp, rows), cells)
            term += dot_nt(cells_of(low_g, zp, rows), cells)
            total = term if total is None else total + term
        point_acc[...] += total

    kept = jnp.where(same, point_acc[...], 0.0).reshape(C, 16, 256).sum(axis=1)
    groups = lax.broadcasted_iota(jnp.int32, (C, 256), 1) // 16
    picks = (groups == lax.broadcasted_iota(jnp.int32, (C, 256), 0)).astype(F32)
    kept = stack([kept, jnp.zeros((128 - C, 256), F32)])
    z_slot = lax.rem(me, 8)
    y_slot = me // 8
    point_z[z_slot] = dot_nt(picks, kept, lax.Precision.HIGHEST)
    small(1, point_z, z_slot, 8, along_z)

    @pl.loop(0, 4)
    def _(group):
        wait_planes(recv_sem, 2, group, recv_c)
        depth_rows(recv_c, rows_ref, group)

    spec = depth_forward(rows_ref, tables["zf"]) * SCALE
    grads[dp, 0] = spec[:, :128]
    grads[dp, 1] = spec[:, 128:]
    small(2, grads, dp, SAMPLES, along_dp)
    mix_adjoint(grads.at[dp], weight, mixed)

    @pl.loop(0, 4)
    def _(group):
        depth_inverse(mixed, tables["zi"], send_d, group)
        send(3, group, send_d, recv_d)

    small_wait(small_recv, 1, point_z, 8)
    point_y[y_slot] = jnp.sum(point_z[...], axis=0)
    small(3, point_y, y_slot, 4, along_y)
    spread(spread_in, (high_g, low_g), local)
    small_wait(small_recv, 3, point_y, 4)
    point_x[dp] = jnp.sum(point_y[...], axis=0)
    small(4, point_x, dp, SAMPLES, along_dp)
    small_wait(small_recv, 0, specs, SAMPLES)
    small_wait(small_recv, 2, grads, SAMPLES)
    weight_grad(specs, grads, spec_grad)
    spec_store = pltpu.make_async_copy(spec_grad, spec_grad_out, store_sem.at[2])
    spec_store.start()

    @pl.loop(0, 4)
    def _(group):
        wait_planes(recv_sem, 3, group, recv_d)
        inverse_y(recv_d, tables["yi"], middle, group)

        @pl.loop(0, ZL // 2)
        def _(zp):
            for k in range(4):
                c = group * 4 + k
                both = inverse_x(middle, tables["xj"], zp, k)
                for zz in range(2):
                    z = 2 * zp + zz
                    grad_in[z, c] = (both[:, zz * Y : (zz + 1) * Y] + local[z, c]).astype(BF)

        pltpu.make_async_copy(
            grad_in.at[:, channels(group)], grad_out.at[0, :, channels(group)], store_sem.at[1]
        ).start()

    small_wait(small_recv, 4, point_x, SAMPLES)
    total = jnp.sum(point_x[...], axis=0)
    point_out[...] = total[:, 0:C] * (1.0 / math.sqrt(CELLS))

    for index, buffer in enumerate((send_a, send_b, send_c, send_d)):
        @pl.loop(0, 4)
        def _(group):
            wait_planes(send_sem, index, group, buffer)

    for index, (buffer, count) in enumerate(
        ((specs, 4), (point_z, 8), (grads, 4), (point_y, 4), (point_x, 4))
    ):
        small_wait(small_send, index, buffer, count)
    spec_store.wait()
    pltpu.make_async_copy(act, act_out.at[0], store_sem.at[0]).wait()
    pltpu.make_async_copy(grad_in, grad_out.at[0], store_sem.at[1]).wait()


def shards(fields, cotangent, spectral_weight, pointwise_weight):
    tables = [jnp.asarray(TABLES[name]) for name in NAMES]
    grid_shape = (ZL, C, X, Y)
    planes = pltpu.VMEM((GROUPS, 4, 16, 128), F32)
    scratch = [pltpu.VMEM(table.shape, BF) for table in tables]
    scratch += [pltpu.VMEM(grid_shape, BF)] * 2
    scratch += [pltpu.VMEM((2, C, C, M * M), BF)]
    scratch += [pltpu.VMEM(grid_shape, BF)] * 4
    scratch += [pltpu.VMEM(grid_shape, F32)]
    scratch += [planes] * 8
    scratch += [pltpu.VMEM((SAMPLES, 2, 128, 128), F32)] * 2
    scratch += [
        pltpu.VMEM((2, 128, 128), F32),
        pltpu.VMEM((512, 512), F32),
        pltpu.VMEM((4, 256, 256), F32),
        pltpu.VMEM((256, 256), BF),
        pltpu.VMEM((256, 256), BF),
        pltpu.VMEM((256, 256), F32),
        pltpu.VMEM((2, C, C, M * M), F32),
        pltpu.VMEM((8, C, 128), F32),
        pltpu.VMEM((4, C, 128), F32),
        pltpu.VMEM((SAMPLES, C, 128), F32),
        pltpu.SemaphoreType.DMA((17,)),
        pltpu.SemaphoreType.DMA((3,)),
        pltpu.SemaphoreType.DMA((4, 4)),
        pltpu.SemaphoreType.DMA((4, 4)),
        pltpu.SemaphoreType.DMA((5,)),
        pltpu.SemaphoreType.DMA((5,)),
    ]
    anywhere = pl.BlockSpec(memory_space=pl.ANY)
    on_chip = pl.BlockSpec(memory_space=pltpu.VMEM)
    return pl.pallas_call(
        step_kernel,
        in_specs=[anywhere] * 3 + [on_chip] + [anywhere] * len(tables),
        out_specs=(anywhere, anywhere, on_chip, anywhere),
        out_shape=(
            jax.ShapeDtypeStruct((1,) + grid_shape, BF),
            jax.ShapeDtypeStruct((1,) + grid_shape, BF),
            jax.ShapeDtypeStruct((C, C), F32),
            jax.ShapeDtypeStruct((2, C, C, M * M), F32),
        ),
        scratch_shapes=scratch,
        compiler_params=pltpu.CompilerParams(
            vmem_limit_bytes=VMEM_LIMIT, collective_id=0, has_side_effects=True
        ),
        name="step",
    )(fields, cotangent, spectral_weight, pointwise_weight, *tables)


def solution(mesh):
    placed = (
        P("dp", "gz", None, None, None),
        P("dp", "gz", None, None, None),
        P(None, None, None, "gz"),
        P(),
    )
    return jax.shard_map(
        shards,
        mesh=mesh,
        in_specs=placed,
        out_specs=(
            P("dp", "gz", None, None, None),
            P("dp", "gz", None, None, None),
            P(),
            P(None, None, None, "gz"),
        ),
        check_vma=False,
    )
```

time: 672 us -> 94.4 us (0.14); the launches traced: 663 us -> 94.2 us
  matrix products: 261 us -> 0 us
  waiting for transfers between devices: 204 us -> 0 us
  local copies, waits for them, and re-layouts: 93.9 us -> 9.39 us
  Pallas kernels: 0 us -> 84.2 us
  blocking collectives: 66.8 us -> 0 us
  other arithmetic: 21.8 us -> 0 us
  between operations: 14.3 us -> 0.65 us
    dot_general x33 -> x0, matrix products: 261 us -> none  [the longest x8 75.5 us: expand(): return jnp.einsum('scpk,zk->szcp', values, table, precision=HIGHEST)]
    reduce_scatter x2 -> x0, waiting for transfers between devices: 164 us -> none  [the longest x1 84.1 us: shards(): lax.psum_scatter(partial_value, 'gz', scatter_dimension=3, tiled=True)]
    pallas_call x0 -> x1, Pallas kernels: none -> 84.2 us  [shards(): pl.pallas_call(step_kernel, in_specs=[anywhere] * 3 + [on_chip] + [anywhe...]
    psum x1 -> x0, blocking collectives: 66.8 us -> none  [shards(): point_total = lax.psum(point_term, ('dp', 'gz'))]
    another operation x16 -> x0, local copies, waits for them, and re-layouts: 62.8 us -> none
    all_gather x2 -> x0, waiting for transfers between devices: 40.5 us -> none  [the longest x1 40.5 us: shards(): whole = lax.all_gather(mixed, 'gz', axis=3, tiled=True)]
    add x2 -> x0, local copies, waits for them, and re-layouts: 12.5 us -> none  [depth_forward(): real_out = contract(planes[0], cos_z) + contract(planes[1], sin_z)]
    another operation x10 -> x0, other arithmetic: 12.2 us -> none  [the longest x2 8.29 us: depth_forward(): return jnp.stack([real_out.reshape(shape), imag_out.reshape(shape)])]
  transfers between devices with their start and end apart: 5 -> 0, of which waited for: 3 -> 0; matrix products, arithmetic and copies ran while one was open for 8% -> 0% of each run, Pallas kernels for 0% -> 0%
where the time goes in v2:
time: 94.4 us; the launch traced here: 94.2 us
  Pallas kernels  84.2 us (89%)
  local copies, waits for them, and re-layouts  9.39 us (10%)
    pallas_call x1, Pallas kernels, shards(): pl.pallas_call(step_kernel, in_specs=[anywhere] * 3 + [on_chip] + [anywhe...  84.2 us
    unnamed x10, local copies, waits for them, and re-layouts  9.39 us

profile of v2, /device:TPU:1, one launch (start us, length us, event | category | flops | bytes accessed | tf_op | source)
XLA Modules:
  0.0 94.2 jit_solution(8685438896344477834)
XLA Ops:
  0.6 84.2 %step.1 = (bf16[1,8,16,128,128]{4,3,2,1,0:T(8,128)(2,1)}, bf16[1,8,16,128,128]{4,3,2,1,0:T(8,128)(2,1)}, f32[16,16]{1,0:T(8,128)}, f32[2,16,16,1024]{3,2,1,0:T(8,128)}) custom-call(bf16[1,8,16,128,128]{4,3,2,1,0:T(8,128)(2,1)} %refs_0_.1, bf16[1,8,16,128,128]{4,3,2,1,0:T(8,128)(2,1)} %refs_1_.1, bf16[2,16,16,1024]{3,2,1,0:T(8,128)(2,1)} %refs_2_.1, ...), custom_call_target="tpu_custom_call" | custom-call | tf_op jit(solution)/shard_map/step/pallas_call | solution.py:579
  84.8 0.0 copy-start
  84.8 4.9 %copy.20 = bf16[1,8,16,128,128]{4,3,2,1,0:T(8,128)(2,1)} copy(bf16[1,8,16,128,128]{4,3,2,1,0:T(8,128)(2,1)} %get-tuple-element.8) | data formatting | bytes 8388608
  89.7 0.0 copy-done
  89.7 0.0 copy-start.2
  89.7 0.0 copy-start.1
  89.8 2.1 %copy.21 = bf16[1,8,16,128,128]{4,3,2,1,0:T(8,128)(2,1)} copy(bf16[1,8,16,128,128]{4,3,2,1,0:T(8,128)(2,1)S(1)} %copy-done) | data formatting | bytes 8388608
  91.9 0.0 copy-done.2
  91.9 0.6 copy.22
  92.5 0.4 copy-done.1
  92.9 1.3 %copy.23 = f32[2,16,16,1024]{3,2,1,0:T(8,128)} copy(f32[2,16,16,1024]{3,2,1,0:T(8,128)S(1)} %copy-done.1) | data formatting | bytes 4194304
Async XLA Ops:
  84.8 5.0 %copy-start = (bf16[1,8,16,128,128]{4,3,2,1,0:T(8,128)(2,1)S(1)}, bf16[1,8,16,128,128]{4,3,2,1,0:T(8,128)(2,1)}, u32[]{:S(2)}) copy-start(bf16[1,8,16,128,128]{4,3,2,1,0:T(8,128)(2,1)} %get-tuple-element.9) | copy-start | bytes 12582916
  89.7 2.1 %copy-start.2 = (f32[16,16]{1,0:T(8,128)S(1)}, f32[16,16]{1,0:T(8,128)}, u32[]{:S(2)}) copy-start(f32[16,16]{1,0:T(8,128)} %get-tuple-element.10) | copy-start | bytes 3076
  89.7 3.1 %copy-start.1 = (f32[2,16,16,1024]{3,2,1,0:T(8,128)S(1)}, f32[2,16,16,1024]{3,2,1,0:T(8,128)}, u32[]{:S(2)}) copy-start(f32[2,16,16,1024]{3,2,1,0:T(8,128)} %get-tuple-element.11) | copy-start | bytes 6291460

commit v3 on v2

--- a/solution.py
+++ b/solution.py
@@ -22,9 +22,10 @@
 SCALE = 1.0 / math.sqrt(X * Y * Z * MODES)
 BF = jnp.bfloat16
 F32 = jnp.float32
-VMEM_LIMIT = 62 * 1024 * 1024
+VMEM_LIMIT = 48 * 1024 * 1024
 K0 = math.sqrt(2.0 / math.pi)
 K1 = K0 * 0.044715
+GRAD = 1.5
 MESH = pl.DeviceIdType.MESH
 
 
@@ -47,6 +48,7 @@
     cos_y, sin_y = wave(Y, ky, np.arange(Y))
     high, low = halves(np.concatenate([cos_y, -sin_y]))
     tables["yf"] = np.concatenate([high, low])
+    high, low = halves(GRAD * np.concatenate([cos_y, -sin_y]))
     tables["yg"] = np.concatenate(
         [np.concatenate([high, high], 1), np.concatenate([low, np.zeros_like(low)], 1)]
     )
@@ -66,7 +68,7 @@
     tables["yi"] = np.stack(
         [np.concatenate([high, high, low, zero]), np.concatenate([high, high, zero, low])]
     )
-    for name, scale in (("xi", SCALE), ("xj", 1.0)):
+    for name, scale in (("xi", 0.5 * SCALE), ("xj", 1.0)):
         high, low = halves(scale * np.concatenate([cos_x, -sin_x]).T)
         tables[name] = np.concatenate([high, high, low], 1)
     cos_z, sin_z = wave(Z, np.arange(Z), np.tile(modes, 4))
@@ -258,7 +260,7 @@
     return side([ref[2 * zp + zz, :, rows, :].reshape(C * 16, Y) for zz in range(2)])
 
 
-def spread(ref, lefts, local):
+def spread(ref, lefts, local, scale):
     @pl.loop(0, X // 16)
     def _(xb):
         rows = pl.ds(pl.multiple_of(xb * 16, 16), 16)
@@ -268,25 +270,26 @@
                 term = dot(ref[...], cells_of(source, zp, rows))
                 total = term if total is None else total + term
             for zz in range(2):
-                local[2 * zp + zz, :, rows, :] = total[:, zz * Y : (zz + 1) * Y].reshape(
-                    C, 16, Y
-                )
+                local[2 * zp + zz, :, rows, :] = (
+                    total[:, zz * Y : (zz + 1) * Y] * scale
+                ).reshape(C, 16, Y)
 
 
 def step_kernel(*refs):
     fields, cotangent, weights, pointwise = refs[:4]
     sources = dict(zip(NAMES, refs[4 : 4 + len(NAMES)]))
     refs = refs[4 + len(NAMES) :]
-    act_out, grad_out, point_out, spec_grad_out = refs[:4]
+    act_out, grad_out, point_out, spec_grad = refs[:4]
+    act, grad_in = act_out.at[0], grad_out.at[0]
     refs = refs[4:]
     tables = dict(zip(NAMES, refs[: len(NAMES)]))
     refs = refs[len(NAMES) :]
     (
-        field, cot, weight, act, grad_in, high_g, low_g, local,
+        field, cot, weight, high_g, low_g, local,
         send_a, recv_a, send_b, recv_b, send_c, recv_c, send_d, recv_d,
-        specs, grads, mixed, rows_ref, middle, spread_out, spread_in, point_acc, spec_grad,
-        point_z, point_y, point_x,
-        load_sem, store_sem, send_sem, recv_sem, small_send, small_recv,
+        specs, grads, mixed, rows_ref, middle, spread_out, spread_in, point_acc,
+        point_z, point_y, point_x, pre,
+        load_sem, send_sem, recv_sem, small_send, small_recv,
     ) = refs
     me = lax.axis_index("gz")
     dp = lax.axis_index("dp")
@@ -402,7 +405,7 @@
         (dot(one_hot, pointwise[...]), spread_in),
     ):
         target[...] = jnp.where(same, dot_nt(left.astype(BF), one_hot), 0.0).astype(BF)
-    spread(spread_out, (field,), local)
+    spread(spread_out, (field,), local, 0.5)
     for name in NAMES:
         if name not in ("yf", "xf"):
             table_load(name).wait()
@@ -431,32 +434,37 @@
         inverse_y(recv_b, tables["yi"], middle, group)
         cot_load(group).wait()
 
-        @pl.loop(0, ZL // 2)
-        def _(zp):
+        for zp in range(ZL // 2 + 2):
             sections = []
             for k in range(4):
                 o = group * 4 + k
-                both = inverse_x(middle, tables["xi"], zp, k)
-                right = []
-                for zz in range(2):
-                    z = 2 * zp + zz
-                    values = both[:, zz * Y : (zz + 1) * Y] + local[z, o]
-                    square = values * values
-                    half = 0.5 + 0.5 * jnp.tanh(values * (K0 + K1 * square))
-                    act[z, o] = (values * half).astype(BF)
-                    slope = half + values * (2.0 * K0 + 6.0 * K1 * square) * (half - half * half)
-                    high, low = split(cot[z, o].astype(F32) * slope)
-                    high_g[z, o] = high
-                    low_g[z, o] = low
-                    right.append(side([high, low]))
-                wide = dot_nt(tables["yg"][...], stack(right))
-                sections.append(wide[:64] + wide[64:])
-            forward_x(sections, tables["xf"], send_c, group, zp)
+                if zp < ZL // 2:
+                    both = inverse_x(middle, tables["xi"], zp, k)
+                    for zz in range(2):
+                        pre[zp % 2, k, zz] = both[:, zz * Y : (zz + 1) * Y]
+                if 1 <= zp <= ZL // 2:
+                    for zz in range(2):
+                        z = 2 * (zp - 1) + zz
+                        values = pre[(zp - 1) % 2, k, zz] + local[z, o]
+                        inner = values * (2.0 * K0 + 8.0 * K1 * (values * values))
+                        wave_t = jnp.tanh(inner)
+                        twice = 1.0 + wave_t
+                        act[z, o] = (values * twice).astype(BF)
+                        slope = 1.0 / 3.0 + (inner - (4.0 / 3.0 * K0) * values) * (1.0 - wave_t)
+                        high, low = split(cot[z, o].astype(F32) * twice * slope)
+                        high_g[z, o] = high
+                        low_g[z, o] = low
+                if 2 <= zp:
+                    right = [
+                        side([high_g[2 * (zp - 2) + zz, o], low_g[2 * (zp - 2) + zz, o]])
+                        for zz in range(2)
+                    ]
+                    wide = dot_nt(tables["yg"][...], stack(right))
+                    sections.append(wide[:64] + wide[64:])
+            if 2 <= zp:
+                forward_x(sections, tables["xf"], send_c, group, zp - 2)
 
         send(2, group, send_c, recv_c)
-        pltpu.make_async_copy(
-            act.at[:, channels(group)], act_out.at[0, :, channels(group)], store_sem.at[0]
-        ).start()
 
     point_acc[...] = jnp.zeros_like(point_acc)
 
@@ -499,15 +507,13 @@
     small_wait(small_recv, 1, point_z, 8)
     point_y[y_slot] = jnp.sum(point_z[...], axis=0)
     small(3, point_y, y_slot, 4, along_y)
-    spread(spread_in, (high_g, low_g), local)
+    spread(spread_in, (high_g, low_g), local, GRAD)
     small_wait(small_recv, 3, point_y, 4)
     point_x[dp] = jnp.sum(point_y[...], axis=0)
     small(4, point_x, dp, SAMPLES, along_dp)
     small_wait(small_recv, 0, specs, SAMPLES)
     small_wait(small_recv, 2, grads, SAMPLES)
     weight_grad(specs, grads, spec_grad)
-    spec_store = pltpu.make_async_copy(spec_grad, spec_grad_out, store_sem.at[2])
-    spec_store.start()
 
     @pl.loop(0, 4)
     def _(group):
@@ -523,13 +529,9 @@
                     z = 2 * zp + zz
                     grad_in[z, c] = (both[:, zz * Y : (zz + 1) * Y] + local[z, c]).astype(BF)
 
-        pltpu.make_async_copy(
-            grad_in.at[:, channels(group)], grad_out.at[0, :, channels(group)], store_sem.at[1]
-        ).start()
-
     small_wait(small_recv, 4, point_x, SAMPLES)
     total = jnp.sum(point_x[...], axis=0)
-    point_out[...] = total[:, 0:C] * (1.0 / math.sqrt(CELLS))
+    point_out[...] = total[:, 0:C] * (GRAD / math.sqrt(CELLS))
 
     for index, buffer in enumerate((send_a, send_b, send_c, send_d)):
         @pl.loop(0, 4)
@@ -540,9 +542,16 @@
         ((specs, 4), (point_z, 8), (grads, 4), (point_y, 4), (point_x, 4))
     ):
         small_wait(small_send, index, buffer, count)
-    spec_store.wait()
-    pltpu.make_async_copy(act, act_out.at[0], store_sem.at[0]).wait()
-    pltpu.make_async_copy(grad_in, grad_out.at[0], store_sem.at[1]).wait()
+
+
+def store_kernel(*refs):
+    copies = [
+        pltpu.make_async_copy(refs[i], refs[4 + i], refs[8].at[i]) for i in range(4)
+    ]
+    for copy in copies:
+        copy.start()
+    for copy in copies:
+        copy.wait()
 
 
 def shards(fields, cotangent, spectral_weight, pointwise_weight):
@@ -552,7 +561,7 @@
     scratch = [pltpu.VMEM(table.shape, BF) for table in tables]
     scratch += [pltpu.VMEM(grid_shape, BF)] * 2
     scratch += [pltpu.VMEM((2, C, C, M * M), BF)]
-    scratch += [pltpu.VMEM(grid_shape, BF)] * 4
+    scratch += [pltpu.VMEM(grid_shape, BF)] * 2
     scratch += [pltpu.VMEM(grid_shape, F32)]
     scratch += [planes] * 8
     scratch += [pltpu.VMEM((SAMPLES, 2, 128, 128), F32)] * 2
@@ -563,12 +572,11 @@
         pltpu.VMEM((256, 256), BF),
         pltpu.VMEM((256, 256), BF),
         pltpu.VMEM((256, 256), F32),
-        pltpu.VMEM((2, C, C, M * M), F32),
         pltpu.VMEM((8, C, 128), F32),
         pltpu.VMEM((4, C, 128), F32),
         pltpu.VMEM((SAMPLES, C, 128), F32),
+        pltpu.VMEM((2, 4, 2, X, Y), F32),
         pltpu.SemaphoreType.DMA((17,)),
-        pltpu.SemaphoreType.DMA((3,)),
         pltpu.SemaphoreType.DMA((4, 4)),
         pltpu.SemaphoreType.DMA((4, 4)),
         pltpu.SemaphoreType.DMA((5,)),
@@ -576,22 +584,32 @@
     ]
     anywhere = pl.BlockSpec(memory_space=pl.ANY)
     on_chip = pl.BlockSpec(memory_space=pltpu.VMEM)
-    return pl.pallas_call(
+    shapes = (
+        jax.ShapeDtypeStruct((1,) + grid_shape, BF),
+        jax.ShapeDtypeStruct((1,) + grid_shape, BF),
+        jax.ShapeDtypeStruct((C, C), F32),
+        jax.ShapeDtypeStruct((2, C, C, M * M), F32),
+    )
+    results = pl.pallas_call(
         step_kernel,
         in_specs=[anywhere] * 3 + [on_chip] + [anywhere] * len(tables),
-        out_specs=(anywhere, anywhere, on_chip, anywhere),
-        out_shape=(
-            jax.ShapeDtypeStruct((1,) + grid_shape, BF),
-            jax.ShapeDtypeStruct((1,) + grid_shape, BF),
-            jax.ShapeDtypeStruct((C, C), F32),
-            jax.ShapeDtypeStruct((2, C, C, M * M), F32),
-        ),
+        out_specs=(on_chip,) * 4,
+        out_shape=tuple(pltpu.VMEM(shape.shape, shape.dtype) for shape in shapes),
         scratch_shapes=scratch,
         compiler_params=pltpu.CompilerParams(
             vmem_limit_bytes=VMEM_LIMIT, collective_id=0, has_side_effects=True
         ),
         name="step",
     )(fields, cotangent, spectral_weight, pointwise_weight, *tables)
+    return pl.pallas_call(
+        store_kernel,
+        in_specs=[on_chip] * 4,
+        out_specs=(anywhere,) * 4,
+        out_shape=shapes,
+        scratch_shapes=[pltpu.SemaphoreType.DMA((4,))],
+        compiler_params=pltpu.CompilerParams(vmem_limit_bytes=1024 * 1024),
+        name="store",
+    )(*results)
 
 
 def solution(mesh):

time: 94.4 us -> 80.3 us (0.85)
  local copies, waits for them, and re-layouts: 9.39 us -> 0 us
  Pallas kernels: 84.2 us -> 79.5 us
    unnamed x10 -> x0, local copies, waits for them, and re-layouts: 9.39 us -> none
    pallas_call x1, Pallas kernels: 84.2 us -> 75.5 us  [shards(): pl.pallas_call(step_kernel, in_specs=[anywhere] * 3 + [on_chip] + [anywhe...]
    pallas_call x0 -> x1, Pallas kernels: none -> 4 us  [shards(): pl.pallas_call(store_kernel, in_specs=[on_chip] * 4, out_specs=(anywhere,...]
where the time goes in v3:
time: 80.3 us; the launch traced here: 80.1 us
  Pallas kernels  79.5 us (99%)
    pallas_call x1, Pallas kernels, shards(): pl.pallas_call(step_kernel, in_specs=[anywhere] * 3 + [on_chip] + [anywhe...  75.5 us
    pallas_call x1, Pallas kernels, shards(): pl.pallas_call(store_kernel, in_specs=[on_chip] * 4, out_specs=(anywhere,...  4 us

profile of v3, /device:TPU:1, one launch (start us, length us, event | category | flops | bytes accessed | tf_op | source)
XLA Modules:
  0.0 80.1 jit_solution(14844952213550998927)
XLA Ops:
  0.6 75.5 %step.1 = (bf16[1,8,16,128,128]{4,3,2,1,0:T(8,128)(2,1)S(1)}, bf16[1,8,16,128,128]{4,3,2,1,0:T(8,128)(2,1)S(1)}, f32[16,16]{1,0:T(8,128)S(1)}, f32[2,16,16,1024]{3,2,1,0:T(8,128)S(1)}) custom-call(bf16[1,8,16,128,128]{4,3,2,1,0:T(8,128)(2,1)} %refs_0_.1, bf16[1,8,16,128,128]{4,3,2,1,0:T(8,128)(2,1)} %refs_1_.1, bf16[2,16,16,1024]{3,2,1,0:T(8,128)(2,1)} %refs_2_.1, ...), custom_call_target="tpu_custom_call" | custom-call | tf_op jit(solution)/shard_map/step/pallas_call | solution.py:593
  76.1 4.0 %store.1 = (bf16[1,8,16,128,128]{4,3,2,1,0:T(8,128)(2,1)}, bf16[1,8,16,128,128]{4,3,2,1,0:T(8,128)(2,1)}, f32[16,16]{1,0:T(8,128)}, f32[2,16,16,1024]{3,2,1,0:T(8,128)}) custom-call(bf16[1,8,16,128,128]{4,3,2,1,0:T(8,128)(2,1)S(1)} %get-tuple-element.8.refs_0_, bf16[1,8,16,128,128]{4,3,2,1,0:T(8,128)(2,1)S(1)} %get-tuple-element.9.refs_1_, ...), custom_call_target="tpu_custom_call" | custom-call | tf_op jit(solution)/shard_map/store/pallas_call | solution.py:604

commit v4 on v3

--- a/solution.py
+++ b/solution.py
@@ -22,7 +22,7 @@
 SCALE = 1.0 / math.sqrt(X * Y * Z * MODES)
 BF = jnp.bfloat16
 F32 = jnp.float32
-VMEM_LIMIT = 48 * 1024 * 1024
+VMEM_LIMIT = 42 * 1024 * 1024
 K0 = math.sqrt(2.0 / math.pi)
 K1 = K0 * 0.044715
 GRAD = 1.5
@@ -84,7 +84,7 @@
 
 
 TABLES = make_tables()
-NAMES = ("yf", "yg", "xf", "yi", "xi", "xj", "zf", "zi")
+NAMES = ("yf", "yg", "xf", "xi", "zf", "zi", "yi", "xj")
 
 
 def dot(a, b):
@@ -138,24 +138,19 @@
         forward_x(sections, xf, out, group, zp)
 
 
-def depth_rows(planes, rows, group):
+def depth_forward(planes, zf, group):
+    halves_in = []
     for part in range(2):
         turned = planes[:, group, part * ZL : (part + 1) * ZL, :].reshape(Z, 128).T
-        for k in range(4):
-            for j in range(4):
-                at = pl.multiple_of(j * 128 + (group * 4 + k) * 8, 8)
-                rows[pl.ds(at, 8), part * 256 : (part + 1) * 256] = turned[
-                    k * 32 + j * 8 : k * 32 + j * 8 + 8
-                ]
-
-
-def depth_forward(rows, zf):
-    which = lax.broadcasted_iota(jnp.int32, (128, 256), 1) // 32 % 4
-    total = None
-    for j in range(4):
-        high, low = split(rows[j * 128 : (j + 1) * 128, :])
-        wide = dot(high, zf[0]) + dot(low, zf[0]) + dot(high, zf[1])
-        total = wide if total is None else jnp.where(which == j, wide, total)
+        halves_in.append(
+            stack([turned[k * 32 + j * 8 : k * 32 + j * 8 + 8] for j in range(4) for k in range(4)])
+        )
+    high, low = split(side(halves_in))
+    wide = dot(high, zf[0]) + dot(low, zf[0]) + dot(high, zf[1])
+    which = lax.broadcasted_iota(jnp.int32, (32, 256), 1) // 32 % 4
+    total = wide[:32]
+    for j in range(1, 4):
+        total = jnp.where(which == j, wide[j * 32 : (j + 1) * 32], total)
     return total
 
 
@@ -163,7 +158,7 @@
     lane = lax.broadcasted_iota(jnp.int32, (8, 128), 1) // 32
     right = []
     for k in range(4):
-        at = pl.ds(pl.multiple_of((group * 4 + k) * 8, 8), 8)
+        at = pl.ds(group * 4 + k, 8, stride=C)
         real_in = spectrum[0, at, :]
         imag_in = spectrum[1, at, :]
         real_in = stack([jnp.where(lane == j, real_in, 0.0) for j in range(4)])
@@ -177,33 +172,36 @@
         ].reshape(GROUPS, ZL, 128)
 
 
-def mix(spec, weight, mixed):
+def mix(spec, weight, mixed, group):
     @pl.loop(0, 8)
     def _(g):
         lanes = pl.ds(pl.multiple_of(g * 128, 128), 128)
-        real_out = jnp.zeros((C, 128), F32)
-        imag_out = jnp.zeros((C, 128), F32)
-        for c in range(C):
+        at = pl.ds(pl.multiple_of(g * C, C), C)
+        real_out = mixed[0, at, :]
+        imag_out = mixed[1, at, :]
+        for k in range(4):
+            c = group * 4 + k
             real_in = spec[0, pl.ds(c * 8 + g, 1), :]
             imag_in = spec[1, pl.ds(c * 8 + g, 1), :]
             wr = weight[0, c, :, lanes].astype(F32)
             wi = weight[1, c, :, lanes].astype(F32)
             real_out += real_in * wr - imag_in * wi
             imag_out += real_in * wi + imag_in * wr
-        mixed[0, pl.ds(g, C, stride=8), :] = real_out
-        mixed[1, pl.ds(g, C, stride=8), :] = imag_out
-
-
-def mix_adjoint(spec, weight, mixed):
+        mixed[0, at, :] = real_out
+        mixed[1, at, :] = imag_out
+
+
+def mix_adjoint(spec, weight, mixed, group):
     @pl.loop(0, 8)
     def _(g):
         lanes = pl.ds(pl.multiple_of(g * 128, 128), 128)
         real_in = spec[0, pl.ds(g, C, stride=8), :]
         imag_in = spec[1, pl.ds(g, C, stride=8), :]
-        for c in range(C):
+        for k in range(4):
+            c = group * 4 + k
             wr = weight[0, c, :, lanes].astype(F32)
             wi = weight[1, c, :, lanes].astype(F32)
-            at = pl.ds(c * 8 + g, 1)
+            at = pl.ds(g * C + c, 1)
             mixed[0, at, :] = jnp.sum(real_in * wr + imag_in * wi, axis=0, keepdims=True)
             mixed[1, at, :] = jnp.sum(imag_in * wr - real_in * wi, axis=0, keepdims=True)
 
@@ -279,15 +277,16 @@
     fields, cotangent, weights, pointwise = refs[:4]
     sources = dict(zip(NAMES, refs[4 : 4 + len(NAMES)]))
     refs = refs[4 + len(NAMES) :]
-    act_out, grad_out, point_out, spec_grad = refs[:4]
-    act, grad_in = act_out.at[0], grad_out.at[0]
-    refs = refs[4:]
-    tables = dict(zip(NAMES, refs[: len(NAMES)]))
-    refs = refs[len(NAMES) :]
+    act_out, grad_in, point_out, spec_grad, local, recv_d, yi, xj = refs[:8]
+    act = act_out.at[0]
+    refs = refs[8:]
+    tables = dict(zip(NAMES, refs[: len(NAMES) - 2]))
+    tables.update(yi=yi, xj=xj)
+    refs = refs[len(NAMES) - 2 :]
     (
-        field, cot, weight, high_g, low_g, local,
-        send_a, recv_a, send_b, recv_b, send_c, recv_c, send_d, recv_d,
-        specs, grads, mixed, rows_ref, middle, spread_out, spread_in, point_acc,
+        field, cot, weight, high_g, low_g,
+        send_a, recv_a, send_b, recv_b, send_c, recv_c, send_d,
+        specs, grads, mixed, middle, spread_out, spread_in, point_acc,
         point_z, point_y, point_x, pre,
         load_sem, send_sem, recv_sem, small_send, small_recv,
     ) = refs
@@ -411,15 +410,18 @@
             table_load(name).wait()
     weight_load.wait()
 
+    def keep_spectrum(target, group, spec):
+        rows = pl.ds(pl.multiple_of(group * 32, 32), 32)
+        target[dp, 0, rows, :] = spec[:, :128]
+        target[dp, 1, rows, :] = spec[:, 128:]
+
+    mixed[...] = jnp.zeros_like(mixed)
+
     @pl.loop(0, 4)
     def _(group):
         wait_planes(recv_sem, 0, group, recv_a)
-        depth_rows(recv_a, rows_ref, group)
-
-    spec = depth_forward(rows_ref, tables["zf"])
-    specs[dp, 0] = spec[:, :128]
-    specs[dp, 1] = spec[:, 128:]
-    mix(specs.at[dp], weight, mixed)
+        keep_spectrum(specs, group, depth_forward(recv_a, tables["zf"], group))
+        mix(specs.at[dp], weight, mixed, group)
 
     @pl.loop(0, 4)
     def _(group):
@@ -468,17 +470,20 @@
 
     point_acc[...] = jnp.zeros_like(point_acc)
 
-    @pl.loop(0, X // 16)
-    def _(xb):
-        rows = pl.ds(pl.multiple_of(xb * 16, 16), 16)
-        total = None
-        for zp in range(ZL // 2):
-            cells = cells_of(field, zp, rows)
-            term = dot_nt(cells_of(high_g, zp, rows), cells)
-            term += dot_nt(cells_of(low_g, zp, rows), cells)
-            total = term if total is None else total + term
-        point_acc[...] += total
-
+    def point_half(first):
+        @pl.loop(first, first + 4)
+        def _(xb):
+            rows = pl.ds(pl.multiple_of(xb * 16, 16), 16)
+            total = None
+            for zp in range(ZL // 2):
+                cells = cells_of(field, zp, rows)
+                term = dot_nt(cells_of(high_g, zp, rows), cells)
+                term += dot_nt(cells_of(low_g, zp, rows), cells)
+                total = term if total is None else total + term
+            point_acc[...] += total
+
+    point_half(0)
+    point_half(4)
     kept = jnp.where(same, point_acc[...], 0.0).reshape(C, 16, 256).sum(axis=1)
     groups = lax.broadcasted_iota(jnp.int32, (C, 256), 1) // 16
     picks = (groups == lax.broadcasted_iota(jnp.int32, (C, 256), 0)).astype(F32)
@@ -488,49 +493,39 @@
     point_z[z_slot] = dot_nt(picks, kept, lax.Precision.HIGHEST)
     small(1, point_z, z_slot, 8, along_z)
 
+
     @pl.loop(0, 4)
     def _(group):
         wait_planes(recv_sem, 2, group, recv_c)
-        depth_rows(recv_c, rows_ref, group)
-
-    spec = depth_forward(rows_ref, tables["zf"]) * SCALE
-    grads[dp, 0] = spec[:, :128]
-    grads[dp, 1] = spec[:, 128:]
+        keep_spectrum(grads, group, depth_forward(recv_c, tables["zf"], group) * SCALE)
+
     small(2, grads, dp, SAMPLES, along_dp)
-    mix_adjoint(grads.at[dp], weight, mixed)
-
-    @pl.loop(0, 4)
-    def _(group):
+
+    def adjoint_group(group):
+        mix_adjoint(grads.at[dp], weight, mixed, group)
         depth_inverse(mixed, tables["zi"], send_d, group)
         send(3, group, send_d, recv_d)
 
+    pl.loop(0, 4)(adjoint_group)
+    spread(spread_in, (high_g, low_g), local, GRAD)
     small_wait(small_recv, 1, point_z, 8)
-    point_y[y_slot] = jnp.sum(point_z[...], axis=0)
-    small(3, point_y, y_slot, 4, along_y)
-    spread(spread_in, (high_g, low_g), local, GRAD)
-    small_wait(small_recv, 3, point_y, 4)
-    point_x[dp] = jnp.sum(point_y[...], axis=0)
+    point_x[dp] = jnp.sum(point_z[...], axis=0)
     small(4, point_x, dp, SAMPLES, along_dp)
     small_wait(small_recv, 0, specs, SAMPLES)
     small_wait(small_recv, 2, grads, SAMPLES)
     weight_grad(specs, grads, spec_grad)
-
-    @pl.loop(0, 4)
+    small_wait(small_recv, 4, point_x, SAMPLES)
+    point_y[y_slot] = jnp.sum(point_x[...], axis=0)
+    small(3, point_y, y_slot, 4, along_y)
+
+    @pl.loop(0, 3)
     def _(group):
         wait_planes(recv_sem, 3, group, recv_d)
-        inverse_y(recv_d, tables["yi"], middle, group)
-
-        @pl.loop(0, ZL // 2)
-        def _(zp):
-            for k in range(4):
-                c = group * 4 + k
-                both = inverse_x(middle, tables["xj"], zp, k)
-                for zz in range(2):
-                    z = 2 * zp + zz
-                    grad_in[z, c] = (both[:, zz * Y : (zz + 1) * Y] + local[z, c]).astype(BF)
-
-    small_wait(small_recv, 4, point_x, SAMPLES)
-    total = jnp.sum(point_x[...], axis=0)
+        input_grad(recv_d, tables["yi"], tables["xj"], middle, local, grad_in, group, group)
+
+    wait_planes(recv_sem, 3, 3, recv_d)
+    small_wait(small_recv, 3, point_y, 4)
+    total = jnp.sum(point_y[...], axis=0)
     point_out[...] = total[:, 0:C] * (GRAD / math.sqrt(CELLS))
 
     for index, buffer in enumerate((send_a, send_b, send_c, send_d)):
@@ -544,12 +539,34 @@
         small_wait(small_send, index, buffer, count)
 
 
-def store_kernel(*refs):
+def input_grad(planes, yi, xj, middle, local, out, group, place):
+    inverse_y(planes, yi, middle, group)
+
+    @pl.loop(0, ZL // 2)
+    def _(zp):
+        for k in range(4):
+            both = inverse_x(middle, xj, zp, k)
+            for zz in range(2):
+                z = 2 * zp + zz
+                values = both[:, zz * Y : (zz + 1) * Y] + local[z, group * 4 + k]
+                out[z, place * 4 + k] = values.astype(BF)
+
+
+def store_kernel(
+    act, grad_in, point, spec_grad, local, planes, yi, xj,
+    act_out, grad_out, point_out, spec_grad_out, middle, last, sems,
+):
     copies = [
-        pltpu.make_async_copy(refs[i], refs[4 + i], refs[8].at[i]) for i in range(4)
+        pltpu.make_async_copy(act, act_out, sems.at[0]),
+        pltpu.make_async_copy(grad_in, grad_out.at[0, :, 0:12], sems.at[1]),
+        pltpu.make_async_copy(point, point_out, sems.at[2]),
+        pltpu.make_async_copy(spec_grad, spec_grad_out, sems.at[3]),
     ]
     for copy in copies:
         copy.start()
+    input_grad(planes, yi, xj, middle, local, last, 3, 0)
+    copies.append(pltpu.make_async_copy(last, grad_out.at[0, :, 12:16], sems.at[4]))
+    copies[4].start()
     for copy in copies:
         copy.wait()
 
@@ -558,16 +575,14 @@
     tables = [jnp.asarray(TABLES[name]) for name in NAMES]
     grid_shape = (ZL, C, X, Y)
     planes = pltpu.VMEM((GROUPS, 4, 16, 128), F32)
-    scratch = [pltpu.VMEM(table.shape, BF) for table in tables]
+    scratch = [pltpu.VMEM(table.shape, BF) for table in tables[:-2]]
     scratch += [pltpu.VMEM(grid_shape, BF)] * 2
     scratch += [pltpu.VMEM((2, C, C, M * M), BF)]
     scratch += [pltpu.VMEM(grid_shape, BF)] * 2
-    scratch += [pltpu.VMEM(grid_shape, F32)]
-    scratch += [planes] * 8
+    scratch += [planes] * 7
     scratch += [pltpu.VMEM((SAMPLES, 2, 128, 128), F32)] * 2
     scratch += [
         pltpu.VMEM((2, 128, 128), F32),
-        pltpu.VMEM((512, 512), F32),
         pltpu.VMEM((4, 256, 256), F32),
         pltpu.VMEM((256, 256), BF),
         pltpu.VMEM((256, 256), BF),
@@ -593,8 +608,17 @@
     results = pl.pallas_call(
         step_kernel,
         in_specs=[anywhere] * 3 + [on_chip] + [anywhere] * len(tables),
-        out_specs=(on_chip,) * 4,
-        out_shape=tuple(pltpu.VMEM(shape.shape, shape.dtype) for shape in shapes),
+        out_specs=(on_chip,) * 8,
+        out_shape=(
+            pltpu.VMEM((1,) + grid_shape, BF),
+            pltpu.VMEM((ZL, 12, X, Y), BF),
+            pltpu.VMEM((C, C), F32),
+            pltpu.VMEM((2, C, C, M * M), F32),
+            pltpu.VMEM(grid_shape, F32),
+            planes,
+            pltpu.VMEM(tables[-2].shape, BF),
+            pltpu.VMEM(tables[-1].shape, BF),
+        ),
         scratch_shapes=scratch,
         compiler_params=pltpu.CompilerParams(
             vmem_limit_bytes=VMEM_LIMIT, collective_id=0, has_side_effects=True
@@ -603,11 +627,15 @@
     )(fields, cotangent, spectral_weight, pointwise_weight, *tables)
     return pl.pallas_call(
         store_kernel,
-        in_specs=[on_chip] * 4,
+        in_specs=[on_chip] * 8,
         out_specs=(anywhere,) * 4,
         out_shape=shapes,
-        scratch_shapes=[pltpu.SemaphoreType.DMA((4,))],
-        compiler_params=pltpu.CompilerParams(vmem_limit_bytes=1024 * 1024),
+        scratch_shapes=[
+            pltpu.VMEM((4, 256, 256), F32),
+            pltpu.VMEM((ZL, 4, X, Y), BF),
+            pltpu.SemaphoreType.DMA((5,)),
+        ],
+        compiler_params=pltpu.CompilerParams(vmem_limit_bytes=8 * 1024 * 1024),
         name="store",
     )(*results)
 

time: 80.3 us -> 74.1 us (0.923)
  Pallas kernels: 79.5 us -> 73.3 us
    pallas_call x1, Pallas kernels: 75.5 us -> 69.3 us  [shards(): pl.pallas_call(step_kernel, in_specs=[anywhere] * 3 + [on_chip] + [anywhe...]
where the time goes in v4:
time: 74.1 us; the launch traced here: 73.9 us
  Pallas kernels  73.3 us (99%)
    pallas_call x1, Pallas kernels, shards(): pl.pallas_call(step_kernel, in_specs=[anywhere] * 3 + [on_chip] + [anywhe...  69.3 us
    pallas_call x1, Pallas kernels, shards(): pl.pallas_call(store_kernel, in_specs=[on_chip] * 8, out_specs=(anywhere,...  4 us

profile of v4, /device:TPU:1, one launch (start us, length us, event | category | flops | bytes accessed | tf_op | source)
XLA Modules:
  0.0 73.9 jit_solution(14000441248435328386)
XLA Ops:
  0.6 69.3 %step.1 = (bf16[1,8,16,128,128]{4,3,2,1,0:T(8,128)(2,1)S(1)}, bf16[8,12,128,128]{3,2,1,0:T(8,128)(2,1)S(1)}, f32[16,16]{1,0:T(8,128)S(1)}, f32[2,16,16,1024]{3,2...) custom-call(bf16[1,8,16,128,128]{4,3,2,1,0:T(8,128)(2,1)} %refs_0_.1, ...), custom_call_target="tpu_custom_call" | custom-call | tf_op jit(solution)/shard_map/step/pallas_call | solution.py:608
  69.9 4.0 %store.1 = (bf16[1,8,16,128,128]{4,3,2,1,0:T(8,128)(2,1)}, bf16[1,8,16,128,128]{4,3,2,1,0:T(8,128)(2,1)}, f32[16,16]{1,0:T(8,128)}, f32[2,16,16,1024]{3,2,1,0:T(8,128)}) custom-call(bf16[1,8,16,128,128]{4,3,2,1,0:T(8,128)(2,1)S(1)} %get-tuple-element.12.act, bf16[8,12,128,128]{3,2,1,0:T(8,128)(2,1)S(1)} %get-tuple-element.13.grad_in, ...), custom_call_target="tpu_custom_call" | custom-call | tf_op jit(solution)/shard_map/store/pallas_call | solution.py:628

commit v5 on v4

--- a/solution.py
+++ b/solution.py
@@ -127,9 +127,10 @@
             ]
 
 
-def field_forward(field, yf, xf, out, group):
+def field_forward(field, yf, xf, out, group, ready=lambda zp: None):
     @pl.loop(0, ZL // 2)
     def _(zp):
+        ready(zp)
         sections = []
         for k in range(4):
             c = group * 4 + k
@@ -288,7 +289,7 @@
         send_a, recv_a, send_b, recv_b, send_c, recv_c, send_d,
         specs, grads, mixed, middle, spread_out, spread_in, point_acc,
         point_z, point_y, point_x, pre,
-        load_sem, send_sem, recv_sem, small_send, small_recv,
+        load_sem, first_sem, send_sem, recv_sem, small_send, small_recv,
     ) = refs
     me = lax.axis_index("gz")
     dp = lax.axis_index("dp")
@@ -327,7 +328,15 @@
     weight_load = pltpu.make_async_copy(weights, weight, load_sem.at[16])
     for name in ("yf", "xf"):
         table_load(name).start()
-    for group in range(4):
+    def first_load(zp):
+        planes = pl.ds(2 * zp, 2)
+        return pltpu.make_async_copy(
+            fields.at[0, planes, 0:4], field.at[planes, 0:4], first_sem.at[zp]
+        )
+
+    for zp in range(ZL // 2):
+        first_load(zp).start()
+    for group in range(1, 4):
         field_load(group).start()
     for name in NAMES:
         if name not in ("yf", "xf"):
@@ -382,8 +391,9 @@
     for name in ("yf", "xf"):
         table_load(name).wait()
 
-    field_load(0).wait()
-    field_forward(field, tables["yf"], tables["xf"], send_a, 0)
+    field_forward(
+        field, tables["yf"], tables["xf"], send_a, 0, lambda zp: first_load(zp).wait()
+    )
     pl.semaphore_wait(barrier, GROUPS - 1 + SAMPLES - 1)
     send(0, 0, send_a, recv_a)
 
@@ -580,9 +590,9 @@
     scratch += [pltpu.VMEM((2, C, C, M * M), BF)]
     scratch += [pltpu.VMEM(grid_shape, BF)] * 2
     scratch += [planes] * 7
-    scratch += [pltpu.VMEM((SAMPLES, 2, 128, 128), F32)] * 2
+    scratch += [pltpu.VMEM((SAMPLES + 1, 2, 128, 128), F32)] * 2
     scratch += [
-        pltpu.VMEM((2, 128, 128), F32),
+        pltpu.VMEM((3, 128, 128), F32),
         pltpu.VMEM((4, 256, 256), F32),
         pltpu.VMEM((256, 256), BF),
         pltpu.VMEM((256, 256), BF),
@@ -592,6 +602,7 @@
         pltpu.VMEM((SAMPLES, C, 128), F32),
         pltpu.VMEM((2, 4, 2, X, Y), F32),
         pltpu.SemaphoreType.DMA((17,)),
+        pltpu.SemaphoreType.DMA((4,)),
         pltpu.SemaphoreType.DMA((4, 4)),
         pltpu.SemaphoreType.DMA((4, 4)),
         pltpu.SemaphoreType.DMA((5,)),

time: 74.1 us -> 74.1 us (level)
  no operation moved by 1% of the time
where the time goes in v5:
time: 74.1 us; the launch traced here: 74 us
  Pallas kernels  73.3 us (99%)
    pallas_call x1, Pallas kernels, shards(): pl.pallas_call(step_kernel, in_specs=[anywhere] * 3 + [on_chip] + [anywhe...  69.4 us
    pallas_call x1, Pallas kernels, shards(): pl.pallas_call(store_kernel, in_specs=[on_chip] * 8, out_specs=(anywhere,...  4 us

profile of v5, /device:TPU:1, one launch (start us, length us, event | category | flops | bytes accessed | tf_op | source)
XLA Modules:
  0.0 74.0 jit_solution(9108116843639664590)
XLA Ops:
  0.6 69.4 %step.1 = (bf16[1,8,16,128,128]{4,3,2,1,0:T(8,128)(2,1)S(1)}, bf16[8,12,128,128]{3,2,1,0:T(8,128)(2,1)S(1)}, f32[16,16]{1,0:T(8,128)S(1)}, f32[2,16,16,1024]{3,2...) custom-call(bf16[1,8,16,128,128]{4,3,2,1,0:T(8,128)(2,1)} %refs_0_.1, ...), custom_call_target="tpu_custom_call" | custom-call | tf_op jit(solution)/shard_map/step/pallas_call | solution.py:619
  70.0 4.0 %store.1 = (bf16[1,8,16,128,128]{4,3,2,1,0:T(8,128)(2,1)}, bf16[1,8,16,128,128]{4,3,2,1,0:T(8,128)(2,1)}, f32[16,16]{1,0:T(8,128)}, f32[2,16,16,1024]{3,2,1,0:T(8,128)}) custom-call(bf16[1,8,16,128,128]{4,3,2,1,0:T(8,128)(2,1)S(1)} %get-tuple-element.12.act, bf16[8,12,128,128]{3,2,1,0:T(8,128)(2,1)S(1)} %get-tuple-element.13.grad_in, ...), custom_call_target="tpu_custom_call" | custom-call | tf_op jit(solution)/shard_map/store/pallas_call | solution.py:639
